TPU v7x, 128 devices: a whole 4x4x4 slice. The times are simulated.
128 devices in a mesh: freq: 4 (over x_hi, core), space: 32 (over z, y, x_lo).
Axes of the slice: x: 4 (x_hi: 2, x_lo: 2; x = x_hi * 2 + x_lo), y: 4, z: 4, core: 2. Of those that a mesh axis runs over, the one named last changes fastest.
Arguments:
- saved_modes: bfloat16 [4, 4, 2, 2, 3, 512, 128, 128], P('freq', None, None, None, None, 'space'), may hold values from -6 to 6
- mode_gains: float32 [4, 4], P('freq'), may hold values from 0.5 to 4
Outputs:
- smoothed_gradient: float32 [512, 128, 128], P('space', 'freq')
All inputs are finite; a program needn't handle non-finite values.
Results may differ from a plain program's by a relative error of at most 0.0003.
Values may be sent and summed in bfloat16 or wider, within the bound.
A program may use at most 256 MiB of HBM per device.

v0:
```python
import jax
import jax.numpy as jnp
from jax import lax
from jax.sharding import PartitionSpec as P

AXIAL = 0.35
CROSS = 0.06


def padded_2(block, sides, width):
    for axis, dim in sides:
        count = lax.axis_size(axis)
        forward = [(i, i + 1) for i in range(count - 1)]
        backward = [(target, source) for source, target in forward]
        low = lax.ppermute(
            lax.slice_in_dim(block, block.shape[dim] - width, None, axis=dim), axis, forward
        )
        high = lax.ppermute(lax.slice_in_dim(block, 0, width, axis=dim), axis, backward)
        block = jnp.concatenate([low, block, high], axis=dim)
    return block


def split_up(x, dim, size):
    dims = x.shape
    tiles = x.reshape(*dims[:dim], size, dims[dim] // size, *dims[dim + 1 :])
    return jnp.moveaxis(tiles, dim, 0)


def sum_at_owner(x, axis, dim):
    tiles = split_up(x, dim, lax.axis_size(axis))
    arrived = lax.all_to_all(tiles, axis, split_axis=0, concat_axis=0, tiled=True)
    return arrived.sum(axis=0)


def shift_z(grid_values, upward):
    zero_plane = jnp.zeros(grid_values.shape[:-1] + (1,), grid_values.dtype)
    if upward:
        return jnp.concatenate([grid_values[..., 1:], zero_plane], axis=-1)
    return jnp.concatenate([zero_plane, grid_values[..., :-1]], axis=-1)


def central_diffs(padded):
    center = padded[:, :, 1:-1, 1:-1]
    along_x = (padded[:, :, 2:, 1:-1] - padded[:, :, :-2, 1:-1]) * 0.5
    along_y = (padded[:, :, 1:-1, 2:] - padded[:, :, 1:-1, :-2]) * 0.5
    along_z = (shift_z(center, True) - shift_z(center, False)) * 0.5
    return (along_x, along_y, along_z)


def strain_dot(grad_forward, grad_adjoint):
    running = jnp.zeros(grad_forward[0].shape[2:], jnp.float32)
    for row_axis in range(3):
        for col_axis in range(3):
            strain_u = 0.5 * (
                grad_forward[row_axis][:, col_axis] + grad_forward[col_axis][:, row_axis]
            )
            strain_v = 0.5 * (
                grad_adjoint[row_axis][:, col_axis] + grad_adjoint[col_axis][:, row_axis]
            )
            running = running + jnp.sum(strain_u * strain_v, axis=0)
    return running


def accumulate(padded, weights, factor):
    mode_count = padded.shape[1]
    pair_total = padded.shape[0] * mode_count
    row_total = padded.shape[6]
    grid_shape = (padded.shape[5] - 2, row_total, padded.shape[7])

    def one_pair(pair_index, running):
        freq_index = pair_index // mode_count
        mode_index = pair_index % mode_count
        mode_pair = lax.dynamic_index_in_dim(padded, freq_index, 0, False)
        mode_pair = lax.dynamic_index_in_dim(mode_pair, mode_index, 0, False).astype(jnp.float32)
        mode_pair = jnp.pad(mode_pair, ((0, 0), (0, 0), (0, 0), (0, 0), (1, 1), (0, 0)))
        weight = lax.dynamic_index_in_dim(
            lax.dynamic_index_in_dim(weights, freq_index, 0, False), mode_index, 0, False
        )
        return running + factor * weight * strain_dot(
            central_diffs(mode_pair[0]), central_diffs(mode_pair[1])
        )

    return lax.fori_loop(0, pair_total, one_pair, jnp.zeros(grid_shape, jnp.float32))


def smooth_step(padded):
    center = padded[1:-1, 1:-1]
    axial = padded[2:, 1:-1] + padded[:-2, 1:-1] - 2.0 * center
    cross = (
        padded[1:-1, 2:]
        + padded[1:-1, :-2]
        + shift_z(center, True)
        + shift_z(center, False)
        - 4.0 * center
    )
    return center + AXIAL * axial + CROSS * cross


def deep_smooth(grid_values):
    slab_rows = grid_values.shape[0]
    band_rows = grid_values.shape[1]
    first_x = lax.axis_index("space") * slab_rows - 3
    total_x = slab_rows * lax.axis_size("space")
    padded = padded_2(grid_values, (("freq", 1), ("space", 0)), 3)
    first_y = lax.axis_index("freq") * band_rows - 3
    total_y = band_rows * lax.axis_size("freq")
    for sweep in range(3):
        padded = smooth_step(padded)
        global_x = first_x + sweep + 1 + jnp.arange(padded.shape[0], dtype=jnp.int32)
        global_y = first_y + sweep + 1 + jnp.arange(padded.shape[1], dtype=jnp.int32)
        valid_x = (global_x >= 0) & (global_x < total_x)
        valid_y = (global_y >= 0) & (global_y < total_y)
        padded = jnp.where(valid_x[:, None, None] & valid_y[None, :, None], padded, 0.0)
    return padded


def smooth(grid_values):
    return deep_smooth(grid_values)


def local(saved_modes, mode_gains):
    mode_count = saved_modes.shape[1]
    freq_total = saved_modes.shape[0] * lax.axis_size("freq")
    factor = -2.0 / (freq_total * mode_count)
    padded = padded_2(saved_modes, (("space", 5),), 1)
    partial_terms = accumulate(padded, mode_gains, factor)
    sensitivity = sum_at_owner(partial_terms, "freq", 1)
    return smooth(sensitivity)


def solution(mesh):
    in_specs = (P("freq", None, None, None, None, "space", None, None), P("freq", None))
    out_specs = P("space", "freq", None)
    return jax.shard_map(local, mesh=mesh, in_specs=in_specs, out_specs=out_specs, check_vma=False)
```

profile of v0, /device:TPU:1, one launch (start us, length us, event | category | flops | bytes accessed | tf_op | source)
XLA Modules:
  0.0 559.0 jit_solution(13774766765793820866)
XLA Ops:
  0.0 3.9 fusion.58
  3.9 4.0 collective-permute-start
  8.0 1.3 collective-permute-start.1
  9.3 0.6 compare_and_fusion.4
  9.9 31.4 %collective-permute-done = bf16[1,4,2,2,3,1,128,128]{7,6,5,4,3,2,1,0:T(8,128)(2,1)S(1)} collective-permute-done((bf16[1,4,2,2,3,1,128,128]{7,6,5,4,3,2,1,0:T(8,128)(2,1)}, bf16[1,4,2,2,3,1,128,128]{7,6,5,4,3,2,1,0:T(8,128)(2,1)S(1)}, u32[]{:S(2)}, u32[]{:S(2)}) %collective-permute-start) | collective-permute-done | bytes 1572896 | tf_op jit(solution)/shard_map/ppermute | solution.py:15
  41.2 35.6 %collective-permute-done.1 = bf16[1,4,2,2,3,1,128,128]{7,6,5,4,3,2,1,0:T(8,128)(2,1)S(1)} collective-permute-done((bf16[1,4,2,2,3,1,128,128]{7,6,5,4,3,2,1,0:T(8,128)(2,1)}, bf16[1,4,2,2,3,1,128,128]{7,6,5,4,3,2,1,0:T(8,128)(2,1)S(1)}, u32[]{:S(2)}, u32[]{:S(2)}) %collective-permute-start.1) | collective-permute-done | bytes 1572896 | tf_op jit(solution)/shard_map/ppermute | solution.py:18
  76.8 18.4 %pad_maximum_fusion = bf16[1,4,2,2,3,18,128,128]{7,6,5,4,3,2,1,0:T(8,128)(2,1)} fusion(bf16[1,4,2,2,3,1,128,128]{7,6,5,4,3,2,1,0:T(8,128)(2,1)S(1)} %collective-permute-done.1, bf16[1,4,2,2,3,16,128,128]{7,6,5,4,3,2,1,0:T(8,128)(2,1)} %param.4, bf16[1,4,2,2,3,1,128,128]{7,6,5,4,3,2,1,0:T(8,128)(2,1)S(1)} %collective-permute-done), kind=kLoop, calls=%fused_computation.52 | loop fusion | flops 28311552 | bytes 56623104 | tf_op jit(solution)/shard_map/concatenate | solution.py:19
  95.2 420.9 %while.16 = (s32[]{:T(128)}, f32[16,128,128]{2,1,0:T(8,128)}, f32[1,4]{1,0:T(1,128)S(1)}, bf16[1,4,2,2,3,18,128,128]{7,6,5,4,3,2,1,0:T(8,128)(2,1)}, s32[]{:T(128)}, /*index=5*/s32[]{:T(128)}, s32[]{:T(128)}, s32[]{:T(128)}) while((s32[]{:T(128)}, f32[16,128,128]{2,1,0:T(8,128)}, f32[1,4]{1,0:T(1,128)S(1)}, ...), condition=%wide.region_7.8_spmd.clone, body=%wide.region_0.7_spmd.clone.sunk | while | flops 42653704 | bytes 329720032 | solution.py:83
  95.2 4.6 dynamic-slice_bitcast_fusion.2
  99.8 8.9 %pad_convert_fusion.2 = f32[2,2,3,18,130,128]{5,4,3,2,1,0:T(8,128)} fusion(bf16[2,2,3,18,128,128]{5,4,3,2,1,0:T(8,128)(2,1)S(1)} %dynamic-slice_bitcast_fusion.2), kind=kLoop, calls=%fused_computation.2.clone.1 | loop fusion | flops 3594240 | bytes 21454848 | tf_op jit(solution)/shard_map/while/body/eval_jaxpr/jit(_pad)/pad | solution.py:75
  108.7 11.6 %slice_bitcast_fusion.3 = (f32[2,3,18,130,128]{4,3,2,1,0:T(8,128)}, f32[2,3,18,130,128]{4,3,2,1,0:T(8,128)}) fusion(f32[2,2,3,18,130,128]{5,4,3,2,1,0:T(8,128)} %pad_convert_fusion.2), kind=kLoop, calls=%fused_computation.1.clone.1 | loop fusion | bytes 28753920 | tf_op jit(solution)/shard_map/while/body/eval_jaxpr/squeeze | solution.py:80
  120.3 17.0 %fusion.68 = (f32[2,3,16,128,127]{4,3,2,1,0:T(8,128)}, f32[2,3,16,128,127]{4,3,2,1,0:T(8,128)}, f32[2,3,16,128,127]{4,3,2,1,0:T(8,128)}, f32[2,3,16,128,127]{4,3,2,1,0:T(8,128)}) fusion(f32[2,3,18,130,128]{4,3,2,1,0:T(8,128)} %get-tuple-element.215, f32[2,3,18,130,128]{4,3,2,1,0:T(8,128)} %get-tuple-element.214), kind=kLoop, calls=%fused_computation.99.clone.1 | loop fusion | bytes 49938432 | tf_op jit(solution)/shard_map/while/body/eval_jaxpr/slice | solution.py:38
  137.3 9.4 %subtract_multiply_fusion.5 = f32[2,3,16,128,128]{4,3,2,1,0:T(8,128)} fusion(f32[2,3,16,128,127]{4,3,2,1,0:T(8,128)} %get-tuple-element.220, f32[2,3,16,128,127]{4,3,2,1,0:T(8,128)} %get-tuple-element.221), kind=kLoop, calls=%fused_computation.13.clone.1 | loop fusion | flops 3145728 | bytes 18776064 | tf_op jit(solution)/shard_map/while/body/eval_jaxpr/mul | solution.py:46
  146.7 0.3 copy-done.1
  147.0 4.4 subtract_multiply_fusion.4
  151.5 27.4 %fusion.67 = (f32[2,3,16,128,128]{4,3,2,1,0:T(8,128)}, f32[2,3,16,128,128]{4,3,2,1,0:T(8,128)}, f32[2,3,16,128,128]{4,3,2,1,0:T(8,128)}, f32[2,3,16,128,128]{4,3,2,1,0:T(8,128)}) fusion(f32[2,3,18,130,128]{4,3,2,1,0:T(8,128)} %get-tuple-element.214, f32[2,3,18,130,128]{4,3,2,1,0:T(8,128)} %get-tuple-element.215), kind=kLoop, calls=%fused_computation.5.clone.1 | loop fusion | flops 12582912 | bytes 75497472 | tf_op jit(solution)/shard_map/while/body/eval_jaxpr/mul | solution.py:45
  178.8 16.5 %fusion.69 = (f32[16,128,128]{2,1,0:T(8,128)S(1)}, f32[16,128,128]{2,1,0:T(8,128)S(1)}, f32[16,128,128]{2,1,0:T(8,128)S(1)}, f32[16,128,128]{2,1,0:T(8,128)}, f3...) fusion(f32[2,3,16,128,128]{4,3,2,1,0:T(8,128)} %get-tuple-element.216, ...), kind=kLoop, calls=%fused_computation.47.clone.1 | loop fusion | flops 17301504 | bytes 44040192 | tf_op jit(solution)/shard_map/while/body/eval_jaxpr/reduce_sum | solution.py:60
  195.4 0.6 fusion.70
  196.0 4.2 select_add_fusion.2
  200.2 4.6 dynamic-slice_bitcast_fusion.2
  204.8 8.9 %pad_convert_fusion.2 = f32[2,2,3,18,130,128]{5,4,3,2,1,0:T(8,128)} fusion(bf16[2,2,3,18,128,128]{5,4,3,2,1,0:T(8,128)(2,1)S(1)} %dynamic-slice_bitcast_fusion.2), kind=kLoop, calls=%fused_computation.2.clone.1 | loop fusion | flops 3594240 | bytes 21454848 | tf_op jit(solution)/shard_map/while/body/eval_jaxpr/jit(_pad)/pad | solution.py:75
  213.7 11.6 %slice_bitcast_fusion.3 = (f32[2,3,18,130,128]{4,3,2,1,0:T(8,128)}, f32[2,3,18,130,128]{4,3,2,1,0:T(8,128)}) fusion(f32[2,2,3,18,130,128]{5,4,3,2,1,0:T(8,128)} %pad_convert_fusion.2), kind=kLoop, calls=%fused_computation.1.clone.1 | loop fusion | bytes 28753920 | tf_op jit(solution)/shard_map/while/body/eval_jaxpr/squeeze | solution.py:80
  225.3 17.0 %fusion.68 = (f32[2,3,16,128,127]{4,3,2,1,0:T(8,128)}, f32[2,3,16,128,127]{4,3,2,1,0:T(8,128)}, f32[2,3,16,128,127]{4,3,2,1,0:T(8,128)}, f32[2,3,16,128,127]{4,3,2,1,0:T(8,128)}) fusion(f32[2,3,18,130,128]{4,3,2,1,0:T(8,128)} %get-tuple-element.215, f32[2,3,18,130,128]{4,3,2,1,0:T(8,128)} %get-tuple-element.214), kind=kLoop, calls=%fused_computation.99.clone.1 | loop fusion | bytes 49938432 | tf_op jit(solution)/shard_map/while/body/eval_jaxpr/slice | solution.py:38
  242.2 9.4 %subtract_multiply_fusion.5 = f32[2,3,16,128,128]{4,3,2,1,0:T(8,128)} fusion(f32[2,3,16,128,127]{4,3,2,1,0:T(8,128)} %get-tuple-element.220, f32[2,3,16,128,127]{4,3,2,1,0:T(8,128)} %get-tuple-element.221), kind=kLoop, calls=%fused_computation.13.clone.1 | loop fusion | flops 3145728 | bytes 18776064 | tf_op jit(solution)/shard_map/while/body/eval_jaxpr/mul | solution.py:46
  251.7 0.3 copy-done.1
  252.0 4.4 subtract_multiply_fusion.4
  256.5 27.4 %fusion.67 = (f32[2,3,16,128,128]{4,3,2,1,0:T(8,128)}, f32[2,3,16,128,128]{4,3,2,1,0:T(8,128)}, f32[2,3,16,128,128]{4,3,2,1,0:T(8,128)}, f32[2,3,16,128,128]{4,3,2,1,0:T(8,128)}) fusion(f32[2,3,18,130,128]{4,3,2,1,0:T(8,128)} %get-tuple-element.214, f32[2,3,18,130,128]{4,3,2,1,0:T(8,128)} %get-tuple-element.215), kind=kLoop, calls=%fused_computation.5.clone.1 | loop fusion | flops 12582912 | bytes 75497472 | tf_op jit(solution)/shard_map/while/body/eval_jaxpr/mul | solution.py:45
  283.8 16.5 %fusion.69 = (f32[16,128,128]{2,1,0:T(8,128)S(1)}, f32[16,128,128]{2,1,0:T(8,128)S(1)}, f32[16,128,128]{2,1,0:T(8,128)S(1)}, f32[16,128,128]{2,1,0:T(8,128)}, f3...) fusion(f32[2,3,16,128,128]{4,3,2,1,0:T(8,128)} %get-tuple-element.216, ...), kind=kLoop, calls=%fused_computation.47.clone.1 | loop fusion | flops 17301504 | bytes 44040192 | tf_op jit(solution)/shard_map/while/body/eval_jaxpr/reduce_sum | solution.py:60
  300.3 0.6 fusion.70
  301.0 4.5 select_add_fusion.2
  305.5 4.6 dynamic-slice_bitcast_fusion.2
  310.1 8.9 %pad_convert_fusion.2 = f32[2,2,3,18,130,128]{5,4,3,2,1,0:T(8,128)} fusion(bf16[2,2,3,18,128,128]{5,4,3,2,1,0:T(8,128)(2,1)S(1)} %dynamic-slice_bitcast_fusion.2), kind=kLoop, calls=%fused_computation.2.clone.1 | loop fusion | flops 3594240 | bytes 21454848 | tf_op jit(solution)/shard_map/while/body/eval_jaxpr/jit(_pad)/pad | solution.py:75
  319.0 11.6 %slice_bitcast_fusion.3 = (f32[2,3,18,130,128]{4,3,2,1,0:T(8,128)}, f32[2,3,18,130,128]{4,3,2,1,0:T(8,128)}) fusion(f32[2,2,3,18,130,128]{5,4,3,2,1,0:T(8,128)} %pad_convert_fusion.2), kind=kLoop, calls=%fused_computation.1.clone.1 | loop fusion | bytes 28753920 | tf_op jit(solution)/shard_map/while/body/eval_jaxpr/squeeze | solution.py:80
  330.5 17.0 %fusion.68 = (f32[2,3,16,128,127]{4,3,2,1,0:T(8,128)}, f32[2,3,16,128,127]{4,3,2,1,0:T(8,128)}, f32[2,3,16,128,127]{4,3,2,1,0:T(8,128)}, f32[2,3,16,128,127]{4,3,2,1,0:T(8,128)}) fusion(f32[2,3,18,130,128]{4,3,2,1,0:T(8,128)} %get-tuple-element.215, f32[2,3,18,130,128]{4,3,2,1,0:T(8,128)} %get-tuple-element.214), kind=kLoop, calls=%fused_computation.99.clone.1 | loop fusion | bytes 49938432 | tf_op jit(solution)/shard_map/while/body/eval_jaxpr/slice | solution.py:38
  347.5 9.4 %subtract_multiply_fusion.5 = f32[2,3,16,128,128]{4,3,2,1,0:T(8,128)} fusion(f32[2,3,16,128,127]{4,3,2,1,0:T(8,128)} %get-tuple-element.220, f32[2,3,16,128,127]{4,3,2,1,0:T(8,128)} %get-tuple-element.221), kind=kLoop, calls=%fused_computation.13.clone.1 | loop fusion | flops 3145728 | bytes 18776064 | tf_op jit(solution)/shard_map/while/body/eval_jaxpr/mul | solution.py:46
  356.9 0.3 copy-done.1
  357.3 4.4 subtract_multiply_fusion.4
  361.7 27.4 %fusion.67 = (f32[2,3,16,128,128]{4,3,2,1,0:T(8,128)}, f32[2,3,16,128,128]{4,3,2,1,0:T(8,128)}, f32[2,3,16,128,128]{4,3,2,1,0:T(8,128)}, f32[2,3,16,128,128]{4,3,2,1,0:T(8,128)}) fusion(f32[2,3,18,130,128]{4,3,2,1,0:T(8,128)} %get-tuple-element.214, f32[2,3,18,130,128]{4,3,2,1,0:T(8,128)} %get-tuple-element.215), kind=kLoop, calls=%fused_computation.5.clone.1 | loop fusion | flops 12582912 | bytes 75497472 | tf_op jit(solution)/shard_map/while/body/eval_jaxpr/mul | solution.py:45
  389.1 16.5 %fusion.69 = (f32[16,128,128]{2,1,0:T(8,128)S(1)}, f32[16,128,128]{2,1,0:T(8,128)S(1)}, f32[16,128,128]{2,1,0:T(8,128)S(1)}, f32[16,128,128]{2,1,0:T(8,128)}, f3...) fusion(f32[2,3,16,128,128]{4,3,2,1,0:T(8,128)} %get-tuple-element.216, ...), kind=kLoop, calls=%fused_computation.47.clone.1 | loop fusion | flops 17301504 | bytes 44040192 | tf_op jit(solution)/shard_map/while/body/eval_jaxpr/reduce_sum | solution.py:60
  405.6 0.6 fusion.70
  406.3 4.5 select_add_fusion.2
  410.8 4.6 dynamic-slice_bitcast_fusion.2
  415.4 8.9 %pad_convert_fusion.2 = f32[2,2,3,18,130,128]{5,4,3,2,1,0:T(8,128)} fusion(bf16[2,2,3,18,128,128]{5,4,3,2,1,0:T(8,128)(2,1)S(1)} %dynamic-slice_bitcast_fusion.2), kind=kLoop, calls=%fused_computation.2.clone.1 | loop fusion | flops 3594240 | bytes 21454848 | tf_op jit(solution)/shard_map/while/body/eval_jaxpr/jit(_pad)/pad | solution.py:75
  424.3 11.6 %slice_bitcast_fusion.3 = (f32[2,3,18,130,128]{4,3,2,1,0:T(8,128)}, f32[2,3,18,130,128]{4,3,2,1,0:T(8,128)}) fusion(f32[2,2,3,18,130,128]{5,4,3,2,1,0:T(8,128)} %pad_convert_fusion.2), kind=kLoop, calls=%fused_computation.1.clone.1 | loop fusion | bytes 28753920 | tf_op jit(solution)/shard_map/while/body/eval_jaxpr/squeeze | solution.py:80
  435.8 17.0 %fusion.68 = (f32[2,3,16,128,127]{4,3,2,1,0:T(8,128)}, f32[2,3,16,128,127]{4,3,2,1,0:T(8,128)}, f32[2,3,16,128,127]{4,3,2,1,0:T(8,128)}, f32[2,3,16,128,127]{4,3,2,1,0:T(8,128)}) fusion(f32[2,3,18,130,128]{4,3,2,1,0:T(8,128)} %get-tuple-element.215, f32[2,3,18,130,128]{4,3,2,1,0:T(8,128)} %get-tuple-element.214), kind=kLoop, calls=%fused_computation.99.clone.1 | loop fusion | bytes 49938432 | tf_op jit(solution)/shard_map/while/body/eval_jaxpr/slice | solution.py:38
  452.8 9.4 %subtract_multiply_fusion.5 = f32[2,3,16,128,128]{4,3,2,1,0:T(8,128)} fusion(f32[2,3,16,128,127]{4,3,2,1,0:T(8,128)} %get-tuple-element.220, f32[2,3,16,128,127]{4,3,2,1,0:T(8,128)} %get-tuple-element.221), kind=kLoop, calls=%fused_computation.13.clone.1 | loop fusion | flops 3145728 | bytes 18776064 | tf_op jit(solution)/shard_map/while/body/eval_jaxpr/mul | solution.py:46
  462.2 0.3 copy-done.1
  462.6 4.4 subtract_multiply_fusion.4
  467.0 27.4 %fusion.67 = (f32[2,3,16,128,128]{4,3,2,1,0:T(8,128)}, f32[2,3,16,128,128]{4,3,2,1,0:T(8,128)}, f32[2,3,16,128,128]{4,3,2,1,0:T(8,128)}, f32[2,3,16,128,128]{4,3,2,1,0:T(8,128)}) fusion(f32[2,3,18,130,128]{4,3,2,1,0:T(8,128)} %get-tuple-element.214, f32[2,3,18,130,128]{4,3,2,1,0:T(8,128)} %get-tuple-element.215), kind=kLoop, calls=%fused_computation.5.clone.1 | loop fusion | flops 12582912 | bytes 75497472 | tf_op jit(solution)/shard_map/while/body/eval_jaxpr/mul | solution.py:45
  494.4 16.5 %fusion.69 = (f32[16,128,128]{2,1,0:T(8,128)S(1)}, f32[16,128,128]{2,1,0:T(8,128)S(1)}, f32[16,128,128]{2,1,0:T(8,128)S(1)}, f32[16,128,128]{2,1,0:T(8,128)}, f3...) fusion(f32[2,3,16,128,128]{4,3,2,1,0:T(8,128)} %get-tuple-element.216, ...), kind=kLoop, calls=%fused_computation.47.clone.1 | loop fusion | flops 17301504 | bytes 44040192 | tf_op jit(solution)/shard_map/while/body/eval_jaxpr/reduce_sum | solution.py:60
  510.9 0.6 fusion.70
  511.6 4.5 select_add_fusion.2
  516.1 2.3 copy.3
  518.4 5.8 %all-to-all-start = ((f32[4,16,32,128]{3,2,1,0:T(8,128)}), f32[4,16,32,128]{3,2,1,0:T(8,128)S(1)}, u32[]{:S(2)}, u32[]{:S(2)}) async-start(f32[4,16,32,128]{3,2,1,0:T(8,128)} %copy.3), calls=%async_computation | async-start | bytes 2097152 | tf_op jit(solution)/shard_map/all_to_all | solution.py:31
  524.4 14.8 %all-to-all-done = f32[4,16,32,128]{3,2,1,0:T(8,128)S(1)} async-done(((f32[4,16,32,128]{3,2,1,0:T(8,128)}), f32[4,16,32,128]{3,2,1,0:T(8,128)S(1)}, u32[]{:S(2)}, u32[]{:S(2)}) %all-to-all-start) | async-done | bytes 1048608 | tf_op jit(solution)/shard_map/all_to_all | solution.py:31
  539.3 2.9 collective-permute-start.2
  542.2 1.9 collective-permute-start.3
  544.1 4.8 collective-permute-done.3
  549.0 2.3 collective-permute-start.4
  551.3 1.3 collective-permute-start.5
  552.7 4.2 collective-permute-done.5
  557.1 0.4 fusion.33
  557.6 0.3 fusion.42
  558.1 0.9 fusion.51
  (34 shorter events, 1.0 us)
Async XLA Ops:
  3.9 37.3 %collective-permute-start = (bf16[1,4,2,2,3,1,128,128]{7,6,5,4,3,2,1,0:T(8,128)(2,1)}, bf16[1,4,2,2,3,1,128,128]{7,6,5,4,3,2,1,0:T(8,128)(2,1)S(1)}, u32[]{:S(2)}, u32[]{:S(2)}) collective-permute-start(bf16[1,4,2,2,3,1,128,128]{7,6,5,4,3,2,1,0:T(8,128)(2,1)} %get-tuple-element.161), channel_id=1, source_target_pairs={{0,1},{1,2},{2,3},{3,4},{4,5},{5,6},{6,7},{7,8},{8,9},{9,10},{10,1... | collective-permute-start | bytes 4718600 | tf_op jit(solution)/shard_map/ppermute | solution.py:15
  8.0 68.9 %collective-permute-start.1 = (bf16[1,4,2,2,3,1,128,128]{7,6,5,4,3,2,1,0:T(8,128)(2,1)}, bf16[1,4,2,2,3,1,128,128]{7,6,5,4,3,2,1,0:T(8,128)(2,1)S(1)}, u32[]{:S(2)}, u32[]{:S(2)}) collective-permute-start(bf16[1,4,2,2,3,1,128,128]{7,6,5,4,3,2,1,0:T(8,128)(2,1)} %get-tuple-element.162), channel_id=1, source_target_pairs={{1,0},{2,1},{3,2},{4,3},{5,4},{6,5},{7,6},{8,7},{9,8},{10,9},{11,1... | collective-permute-start | bytes 4718600 | tf_op jit(solution)/shard_map/ppermute | solution.py:18
  9.9 85.4 %copy-start.3 = (f32[1,4]{1,0:T(1,128)S(1)}, f32[1,4]{1,0:T(1,128)}, u32[]{:S(2)}) copy-start(f32[1,4]{1,0:T(1,128)} %param.5) | copy-start | bytes 52
  95.2 457.4 %copy-start.2 = (pred[32]{0:T(512)(128)(4,1)S(1)}, pred[32]{0:T(512)(128)(4,1)}, u32[]{:S(2)}) copy-start(pred[32]{0:T(512)(128)(4,1)} %compare_and_fusion.4) | copy-start | bytes 100
  137.3 9.4 %copy-start = (f32[2,3,16,128,127]{4,3,2,1,0:T(8,128)S(1)}, f32[2,3,16,128,127]{4,3,2,1,0:T(8,128)}, u32[]{:S(2)}) copy-start(f32[2,3,16,128,127]{4,3,2,1,0:T(8,128)} %get-tuple-element.218) | copy-start | bytes 18726916 | tf_op jit(solution)/shard_map/while
  137.3 9.8 %copy-start.1 = (f32[2,3,16,128,127]{4,3,2,1,0:T(8,128)S(1)}, f32[2,3,16,128,127]{4,3,2,1,0:T(8,128)}, u32[]{:S(2)}) copy-start(f32[2,3,16,128,127]{4,3,2,1,0:T(8,128)} %get-tuple-element.219) | copy-start | bytes 18726916 | tf_op jit(solution)/shard_map/while
  242.2 9.4 %copy-start = (f32[2,3,16,128,127]{4,3,2,1,0:T(8,128)S(1)}, f32[2,3,16,128,127]{4,3,2,1,0:T(8,128)}, u32[]{:S(2)}) copy-start(f32[2,3,16,128,127]{4,3,2,1,0:T(8,128)} %get-tuple-element.218) | copy-start | bytes 18726916 | tf_op jit(solution)/shard_map/while
  242.2 9.8 %copy-start.1 = (f32[2,3,16,128,127]{4,3,2,1,0:T(8,128)S(1)}, f32[2,3,16,128,127]{4,3,2,1,0:T(8,128)}, u32[]{:S(2)}) copy-start(f32[2,3,16,128,127]{4,3,2,1,0:T(8,128)} %get-tuple-element.219) | copy-start | bytes 18726916 | tf_op jit(solution)/shard_map/while
  347.5 9.4 %copy-start = (f32[2,3,16,128,127]{4,3,2,1,0:T(8,128)S(1)}, f32[2,3,16,128,127]{4,3,2,1,0:T(8,128)}, u32[]{:S(2)}) copy-start(f32[2,3,16,128,127]{4,3,2,1,0:T(8,128)} %get-tuple-element.218) | copy-start | bytes 18726916 | tf_op jit(solution)/shard_map/while
  347.5 9.8 %copy-start.1 = (f32[2,3,16,128,127]{4,3,2,1,0:T(8,128)S(1)}, f32[2,3,16,128,127]{4,3,2,1,0:T(8,128)}, u32[]{:S(2)}) copy-start(f32[2,3,16,128,127]{4,3,2,1,0:T(8,128)} %get-tuple-element.219) | copy-start | bytes 18726916 | tf_op jit(solution)/shard_map/while
  452.8 9.4 %copy-start = (f32[2,3,16,128,127]{4,3,2,1,0:T(8,128)S(1)}, f32[2,3,16,128,127]{4,3,2,1,0:T(8,128)}, u32[]{:S(2)}) copy-start(f32[2,3,16,128,127]{4,3,2,1,0:T(8,128)} %get-tuple-element.218) | copy-start | bytes 18726916 | tf_op jit(solution)/shard_map/while
  452.8 9.8 %copy-start.1 = (f32[2,3,16,128,127]{4,3,2,1,0:T(8,128)S(1)}, f32[2,3,16,128,127]{4,3,2,1,0:T(8,128)}, u32[]{:S(2)}) copy-start(f32[2,3,16,128,127]{4,3,2,1,0:T(8,128)} %get-tuple-element.219) | copy-start | bytes 18726916 | tf_op jit(solution)/shard_map/while
  518.4 20.8 %all-to-all-start = ((f32[4,16,32,128]{3,2,1,0:T(8,128)}), f32[4,16,32,128]{3,2,1,0:T(8,128)S(1)}, u32[]{:S(2)}, u32[]{:S(2)}) async-start(f32[4,16,32,128]{3,2,1,0:T(8,128)} %copy.3), calls=%async_computation | async-start | bytes 2097152 | tf_op jit(solution)/shard_map/all_to_all | solution.py:31
  539.3 4.8 collective-permute-start.2
  542.2 6.7 %collective-permute-start.3 = (f32[16,3,128]{2,1,0:T(4,128)S(1)}, f32[16,3,128]{2,1,0:T(4,128)S(1)}, u32[]{:S(2)}, u32[]{:S(2)}) collective-permute-start(f32[16,3,128]{2,1,0:T(4,128)S(1)} %get-tuple-element.172), channel_id=1, source_target_pairs={{32,0},{64,32},{96,64},{33,1},{65,33},{97,65},{34,2},{66,34},{98,6... | collective-permute-start | bytes 73736 | tf_op jit(solution)/shard_map/ppermute | solution.py:18
  549.0 3.7 collective-permute-start.4
  551.3 5.6 collective-permute-start.5
where the time goes:
time: 562 us; the launch traced here: 559 us
  other arithmetic  308 us (55%)
  local copies, waits for them, and re-layouts  141 us (25%)
  waiting for transfers between devices  90.7 us (16%)
  starting transfers between devices  19.5 us (3%)
    mul x4, other arithmetic, central_diffs(): along_y = (padded[:, :, 1:-1, 2:] - padded[:, :, 1:-1, :-2]) * 0.5  109 us
    slice x7, local copies, waits for them, and re-layouts, shift_z(): return jnp.concatenate([grid_values[..., 1:], zero_plane], axis=-1)  68.4 us
    reduce_sum x4, other arithmetic, strain_dot(): running = running + jnp.sum(strain_u * strain_v, axis=0)  66.1 us
    mul x8, other arithmetic, central_diffs(): along_z = (shift_z(center, True) - shift_z(center, False)) * 0.5  55.4 us
    squeeze x4, local copies, waits for them, and re-layouts, one_pair(): mode_pair[0]  46.3 us
    ppermute x3, waiting for transfers between devices, padded_2(): lax.ppermute(lax.slice_in_dim(block, 0, width, axis=dim), axis, backward)  44.6 us
    pad x4, other arithmetic, one_pair(): jnp.pad(mode_pair, ((0, 0), (0, 0), (0, 0), (0, 0), (1, 1), (0, 0)))  35.6 us
    ppermute x3, waiting for transfers between devices, padded_2(): lax.ppermute(lax.slice_in_dim(block, block.shape[dim] - width, None, axis...  31.4 us
  transfers between devices with their start and end apart: 7, of which 5 were waited for; matrix products, arithmetic and copies ran while one was open for 0% of the time, Pallas kernels for 0%

commit v1 on v0

--- a/solution.py
+++ b/solution.py
@@ -1,6 +1,10 @@
+import functools
+
 import jax
 import jax.numpy as jnp
 from jax import lax
+from jax.experimental import pallas as pl
+from jax.experimental.pallas import tpu as pltpu
 from jax.sharding import PartitionSpec as P
 
 AXIAL = 0.35
@@ -38,49 +42,139 @@
         return jnp.concatenate([grid_values[..., 1:], zero_plane], axis=-1)
     return jnp.concatenate([zero_plane, grid_values[..., :-1]], axis=-1)
 
-
-def central_diffs(padded):
-    center = padded[:, :, 1:-1, 1:-1]
-    along_x = (padded[:, :, 2:, 1:-1] - padded[:, :, :-2, 1:-1]) * 0.5
-    along_y = (padded[:, :, 1:-1, 2:] - padded[:, :, 1:-1, :-2]) * 0.5
-    along_z = (shift_z(center, True) - shift_z(center, False)) * 0.5
-    return (along_x, along_y, along_z)
-
-
-def strain_dot(grad_forward, grad_adjoint):
-    running = jnp.zeros(grad_forward[0].shape[2:], jnp.float32)
-    for row_axis in range(3):
-        for col_axis in range(3):
-            strain_u = 0.5 * (
-                grad_forward[row_axis][:, col_axis] + grad_forward[col_axis][:, row_axis]
-            )
-            strain_v = 0.5 * (
-                grad_adjoint[row_axis][:, col_axis] + grad_adjoint[col_axis][:, row_axis]
-            )
-            running = running + jnp.sum(strain_u * strain_v, axis=0)
-    return running
-
-
-def accumulate(padded, weights, factor):
-    mode_count = padded.shape[1]
-    pair_total = padded.shape[0] * mode_count
-    row_total = padded.shape[6]
-    grid_shape = (padded.shape[5] - 2, row_total, padded.shape[7])
-
-    def one_pair(pair_index, running):
-        freq_index = pair_index // mode_count
-        mode_index = pair_index % mode_count
-        mode_pair = lax.dynamic_index_in_dim(padded, freq_index, 0, False)
-        mode_pair = lax.dynamic_index_in_dim(mode_pair, mode_index, 0, False).astype(jnp.float32)
-        mode_pair = jnp.pad(mode_pair, ((0, 0), (0, 0), (0, 0), (0, 0), (1, 1), (0, 0)))
-        weight = lax.dynamic_index_in_dim(
-            lax.dynamic_index_in_dim(weights, freq_index, 0, False), mode_index, 0, False
-        )
-        return running + factor * weight * strain_dot(
-            central_diffs(mode_pair[0]), central_diffs(mode_pair[1])
-        )
-
-    return lax.fori_loop(0, pair_total, one_pair, jnp.zeros(grid_shape, jnp.float32))
+MESH = pl.DeviceIdType.MESH
+
+
+def diff_matrices(count):
+    row = lax.broadcasted_iota(jnp.int32, (count, count), 0)
+    col = lax.broadcasted_iota(jnp.int32, (count, count), 1)
+    upper = (col == row + 1).astype(jnp.float32)
+    lower = (col + 1 == row).astype(jnp.float32)
+    along_rows = (upper - lower).astype(jnp.bfloat16)
+    along_cols = (lower - upper).astype(jnp.bfloat16)
+    return along_rows, along_cols
+
+
+def strain_parts(field, x, diff_y, diff_z, low, high):
+    center = [field[c, x] for c in range(3)]
+    after = [field[c, x + 1].astype(jnp.float32) for c in range(3)]
+    before = [field[c, x - 1].astype(jnp.float32) for c in range(3)]
+    if high is not None:
+        after = [value * high for value in after]
+    if low is not None:
+        before = [value * low for value in before]
+    dx = [after[c] - before[c] for c in range(3)]
+    dy = [jnp.dot(diff_y, center[c], preferred_element_type=jnp.float32) for c in range(3)]
+    dz = [jnp.dot(center[c], diff_z, preferred_element_type=jnp.float32) for c in range(3)]
+    return (dx[0], dy[1], dz[2], dx[1] + dy[0], dx[2] + dz[0], dy[2] + dz[1])
+
+
+def pair_term(forward, adjoint, x, diff_y, diff_z, low=None, high=None):
+    eu = strain_parts(forward, x, diff_y, diff_z, low, high)
+    ev = strain_parts(adjoint, x, diff_y, diff_z, low, high)
+    straight = eu[0] * ev[0] + eu[1] * ev[1] + eu[2] * ev[2]
+    shear = eu[3] * ev[3] + eu[4] * ev[4] + eu[5] * ev[5]
+    return straight + 0.5 * shear
+
+
+def strain_kernel(space, factor, modes, gains, out, buf, ymat, zmat, load_sem, send_sem, recv_sem):
+    mode_count = modes.shape[1]
+    planes = modes.shape[5]
+    me = lax.axis_index("space")
+    above = lax.rem(me + 1, space)
+    below = lax.rem(me + space - 1, space)
+
+    def load(m):
+        return pltpu.make_async_copy(
+            modes.at[0, m], buf.at[m, :, :, :, pl.ds(1, planes)], load_sem.at[m]
+        )
+
+    def halo(c, side):
+        m, part = c // 2, lax.rem(c, 2)
+        plane, slot, target = (planes - 1, 0, above) if side == 0 else (0, planes + 1, below)
+        return pltpu.make_async_remote_copy(
+            src_ref=modes.at[0, m, :, part, :, plane],
+            dst_ref=buf.at[m, :, part, :, slot],
+            send_sem=send_sem.at[side, c],
+            recv_sem=recv_sem.at[side, c],
+            device_id={"space": target},
+            device_id_type=MESH,
+        )
+
+    load(0).start()
+    barrier = pltpu.get_barrier_semaphore()
+    for target in (above, below):
+        pl.semaphore_signal(barrier, inc=1, device_id={"space": target}, device_id_type=MESH)
+    pl.semaphore_wait(barrier, 2)
+
+    @pl.loop(0, 2 * mode_count)
+    def _(c):
+        halo(c, 0).start()
+        halo(c, 1).start()
+
+    @pl.loop(1, mode_count)
+    def _(m):
+        load(m).start()
+
+    diff_y, diff_z = diff_matrices(modes.shape[6])
+    ymat[...] = diff_y
+    zmat[...] = diff_z
+    out[...] = jnp.zeros_like(out)
+
+    def term(m, part, x, low=None, high=None):
+        return pair_term(
+            buf.at[m, 0, part], buf.at[m, 1, part], x, ymat[...], zmat[...], low, high
+        )
+
+    @pl.loop(0, mode_count)
+    def _(m):
+        load(m).wait()
+        weight = gains[0, m] * (0.25 * factor)
+
+        @pl.loop(2, planes)
+        def _(x):
+            out[x - 1] += weight * (term(m, 0, x) + term(m, 1, x))
+
+    low = jnp.where(me > 0, 1.0, 0.0).astype(jnp.float32)
+    high = jnp.where(me < space - 1, 1.0, 0.0).astype(jnp.float32)
+
+    @pl.loop(0, 2 * mode_count)
+    def _(c):
+        m, part = c // 2, lax.rem(c, 2)
+        weight = gains[0, m] * (0.25 * factor)
+        halo(c, 0).wait_recv()
+        out[0] += weight * term(m, part, 1, low=low)
+        halo(c, 1).wait_recv()
+        out[planes - 1] += weight * term(m, part, planes, high=high)
+
+    @pl.loop(0, 2 * mode_count)
+    def _(c):
+        halo(c, 0).wait_send()
+        halo(c, 1).wait_send()
+
+
+def partial_sensitivity(saved_modes, mode_gains, factor):
+    _, mode_count, pair, parts, comps, planes, rows, cols = saved_modes.shape
+    return pl.pallas_call(
+        functools.partial(strain_kernel, lax.axis_size("space"), factor),
+        out_shape=jax.ShapeDtypeStruct((planes, rows, cols), jnp.float32),
+        in_specs=[
+            pl.BlockSpec(memory_space=pl.ANY),
+            pl.BlockSpec(memory_space=pltpu.SMEM),
+        ],
+        out_specs=pl.BlockSpec(memory_space=pltpu.VMEM),
+        scratch_shapes=[
+            pltpu.VMEM((mode_count, pair, parts, comps, planes + 2, rows, cols), jnp.bfloat16),
+            pltpu.VMEM((rows, rows), jnp.bfloat16),
+            pltpu.VMEM((cols, cols), jnp.bfloat16),
+            pltpu.SemaphoreType.DMA((mode_count,)),
+            pltpu.SemaphoreType.DMA((2, 2 * mode_count)),
+            pltpu.SemaphoreType.DMA((2, 2 * mode_count)),
+        ],
+        compiler_params=pltpu.CompilerParams(
+            collective_id=0, has_side_effects=True, vmem_limit_bytes=60 << 20
+        ),
+    )(saved_modes, mode_gains)
 
 
 def smooth_step(padded):
@@ -122,8 +216,7 @@
     mode_count = saved_modes.shape[1]
     freq_total = saved_modes.shape[0] * lax.axis_size("freq")
     factor = -2.0 / (freq_total * mode_count)
-    padded = padded_2(saved_modes, (("space", 5),), 1)
-    partial_terms = accumulate(padded, mode_gains, factor)
+    partial_terms = partial_sensitivity(saved_modes, mode_gains, factor)
     sensitivity = sum_at_owner(partial_terms, "freq", 1)
     return smooth(sensitivity)
 

time: 562 us -> 119 us (0.21)
  other arithmetic: 308 us -> 2.04 us
  local copies, waits for them, and re-layouts: 141 us -> 2.84 us
  Pallas kernels: 0 us -> 77 us
  waiting for transfers between devices: 90.7 us -> 23.1 us
  starting transfers between devices: 19.5 us -> 12.9 us
    mul x16 -> x0, other arithmetic: 167 us -> none  [the longest x4 109 us: central_diffs(): along_y = (padded[:, :, 1:-1, 2:] - padded[:, :, 1:-1, :-2]) * 0.5]
    pallas_call x0 -> x1, Pallas kernels: none -> 77 us  [partial_sensitivity(): pl.pallas_call(functools.partial(strain_kernel, lax.axis_size('space'), f...]
    slice x7 -> x3, local copies, waits for them, and re-layouts: 68.4 us -> 0.48 us  [shift_z(): return jnp.concatenate([grid_values[..., 1:], zero_plane], axis=-1)]
    reduce_sum x4 -> x0, other arithmetic: 66.1 us -> none  [strain_dot(): running = running + jnp.sum(strain_u * strain_v, axis=0)]
    squeeze x4 -> x0, local copies, waits for them, and re-layouts: 46.3 us -> none  [one_pair(): mode_pair[0]]
    ppermute x3 -> x2, waiting for transfers between devices: 44.6 us -> 8.37 us  [padded_2(): lax.ppermute(lax.slice_in_dim(block, 0, width, axis=dim), axis, backward)]
    pad x4 -> x0, other arithmetic: 35.6 us -> none  [one_pair(): jnp.pad(mode_pair, ((0, 0), (0, 0), (0, 0), (0, 0), (1, 1), (0, 0)))]
    ppermute x3 -> x2, waiting for transfers between devices: 31.4 us -> 0.01 us  [padded_2(): lax.ppermute(lax.slice_in_dim(block, block.shape[dim] - width, None, axis...]
  transfers between devices with their start and end apart: 7 -> 5, of which waited for: 5 -> 3; matrix products, arithmetic and copies ran while one was open for 0% -> 0% of each run, Pallas kernels for 0% -> 0%
where the time goes in v1:
time: 119 us; the launch traced here: 118 us
  Pallas kernels  77 us (65%)
  waiting for transfers between devices  23.1 us (19%)
  starting transfers between devices  12.9 us (11%)
  local copies, waits for them, and re-layouts  2.84 us (2%)
  other arithmetic  2.04 us (2%)
    pallas_call x1, Pallas kernels, partial_sensitivity(): pl.pallas_call(functools.partial(strain_kernel, lax.axis_size('space'), f...  77 us
    all_to_all x1, waiting for transfers between devices, sum_at_owner(): lax.all_to_all(tiles, axis, split_axis=0, concat_axis=0, tiled=True)  14.8 us
    ppermute x2, waiting for transfers between devices, padded_2(): lax.ppermute(lax.slice_in_dim(block, 0, width, axis=dim), axis, backward)  8.37 us
    all_to_all x1, starting transfers between devices, sum_at_owner(): lax.all_to_all(tiles, axis, split_axis=0, concat_axis=0, tiled=True)  5.53 us
    ppermute x2, starting transfers between devices, padded_2(): lax.ppermute(lax.slice_in_dim(block, block.shape[dim] - width, None, axis...  4.17 us
    ppermute x2, starting transfers between devices, padded_2(): lax.ppermute(lax.slice_in_dim(block, 0, width, axis=dim), axis, backward)  3.21 us
  transfers between devices with their start and end apart: 5, of which 3 were waited for; matrix products, arithmetic and copies ran while one was open for 0% of the time, Pallas kernels for 0%

profile of v1, /device:TPU:1, one launch (start us, length us, event | category | flops | bytes accessed | tf_op | source)
XLA Modules:
  0.0 118.1 jit_solution(3206797931690404343)
XLA Ops:
  0.0 77.0 %shard_map.28 = f32[16,128,128]{2,1,0:T(8,128)} custom-call(bf16[1,4,2,2,3,16,128,128]{7,6,5,4,3,2,1,0:T(8,128)(2,1)} %modes.1, f32[1,4]{1,0:T(1,128)} %gains.1), custom_call_target="tpu_custom_call" | custom-call | tf_op jit(solution)/shard_map/pallas_call | solution.py:158
  77.0 2.3 %copy.5 = f32[16,4,32,128]{3,2,0,1:T(8,128)} copy(f32[16,4,32,128]{3,2,1,0:T(8,128)} %bitcast.4) | data formatting | bytes 2097152 | tf_op jit(solution)/shard_map/reshape | solution.py:29
  79.4 5.5 %all-to-all-start = ((f32[4,16,32,128]{3,2,1,0:T(8,128)}), f32[4,16,32,128]{3,2,1,0:T(8,128)S(1)}, u32[]{:S(2)}, u32[]{:S(2)}) async-start(f32[4,16,32,128]{3,2,1,0:T(8,128)} %bitcast.3), calls=%async_computation | async-start | bytes 2097152 | tf_op jit(solution)/shard_map/all_to_all | solution.py:35
  85.0 0.1 broadcast_and_fusion
  85.0 0.1 broadcast_and_fusion.1
  85.1 14.8 %all-to-all-done = f32[4,16,32,128]{3,2,1,0:T(8,128)S(1)} async-done(((f32[4,16,32,128]{3,2,1,0:T(8,128)}), f32[4,16,32,128]{3,2,1,0:T(8,128)S(1)}, u32[]{:S(2)}, u32[]{:S(2)}) %all-to-all-start) | async-done | bytes 1048608 | tf_op jit(solution)/shard_map/all_to_all | solution.py:35
  99.9 0.1 reduce_sum.9
  100.0 2.9 %collective-permute-start = (f32[16,3,128]{2,1,0:T(4,128)S(1)}, f32[16,3,128]{2,1,0:T(4,128)S(1)}, u32[]{:S(2)}, u32[]{:S(2)}) collective-permute-start(f32[16,3,128]{2,1,0:T(4,128)S(1)} %get-tuple-element.13), channel_id=1, source_target_pairs={{0,32},{32,64},{64,96},{1,33},{33,65},{65,97},{2,34},{34,66},{66,9... | collective-permute-start | bytes 73736 | tf_op jit(solution)/shard_map/ppermute | solution.py:19
  102.9 1.9 %collective-permute-start.1 = (f32[16,3,128]{2,1,0:T(4,128)S(1)}, f32[16,3,128]{2,1,0:T(4,128)S(1)}, u32[]{:S(2)}, u32[]{:S(2)}) collective-permute-start(f32[16,3,128]{2,1,0:T(4,128)S(1)} %get-tuple-element.14), channel_id=1, source_target_pairs={{32,0},{64,32},{96,64},{33,1},{65,33},{97,65},{34,2},{66,34},{98,6... | collective-permute-start | bytes 73736 | tf_op jit(solution)/shard_map/ppermute | solution.py:22
  104.8 0.0 collective-permute-done
  104.8 4.8 %collective-permute-done.1 = f32[16,3,128]{2,1,0:T(4,128)S(1)} collective-permute-done((f32[16,3,128]{2,1,0:T(4,128)S(1)}, f32[16,3,128]{2,1,0:T(4,128)S(1)}, u32[]{:S(2)}, u32[]{:S(2)}) %collective-permute-start.1) | collective-permute-done | bytes 24608 | tf_op jit(solution)/shard_map/ppermute | solution.py:22
  109.6 1.3 %collective-permute-start.2 = (f32[3,38,128]{2,1,0:T(8,128)S(1)}, f32[3,38,128]{2,1,0:T(8,128)S(1)}, u32[]{:S(2)}, u32[]{:S(2)}) collective-permute-start(f32[3,38,128]{2,1,0:T(8,128)S(1)} %get-tuple-element.11), channel_id=1, source_target_pairs={{0,1},{1,2},{2,3},{3,4},{4,5},{5,6},{6,7},{7,8},{8,9},{9,10},{10,1... | collective-permute-start | bytes 175112 | tf_op jit(solution)/shard_map/ppermute | solution.py:19
  110.9 1.3 %collective-permute-start.3 = (f32[3,38,128]{2,1,0:T(8,128)S(1)}, f32[3,38,128]{2,1,0:T(8,128)S(1)}, u32[]{:S(2)}, u32[]{:S(2)}) collective-permute-start(f32[3,38,128]{2,1,0:T(8,128)S(1)} %get-tuple-element.12), channel_id=1, source_target_pairs={{1,0},{2,1},{3,2},{4,3},{5,4},{6,5},{7,6},{8,7},{9,8},{10,9},{11,1... | collective-permute-start | bytes 175112 | tf_op jit(solution)/shard_map/ppermute | solution.py:22
  112.2 0.1 broadcast_and_fusion.2
  112.3 0.0 collective-permute-done.2
  112.3 3.6 %collective-permute-done.3 = f32[3,38,128]{2,1,0:T(8,128)S(1)} collective-permute-done((f32[3,38,128]{2,1,0:T(8,128)S(1)}, f32[3,38,128]{2,1,0:T(8,128)S(1)}, u32[]{:S(2)}, u32[]{:S(2)}) %collective-permute-start.3) | collective-permute-done | bytes 58400 | tf_op jit(solution)/shard_map/ppermute | solution.py:22
  115.9 0.1 pad_maximum_fusion
  115.9 0.2 fusion.27
  116.1 0.4 fusion.5
  116.5 0.2 fusion.28
  116.6 0.3 fusion.14
  117.0 0.1 fusion.29
  117.1 0.9 fusion.23
  (8 shorter events, 0.1 us)
Async XLA Ops:
  79.4 20.5 %all-to-all-start = ((f32[4,16,32,128]{3,2,1,0:T(8,128)}), f32[4,16,32,128]{3,2,1,0:T(8,128)S(1)}, u32[]{:S(2)}, u32[]{:S(2)}) async-start(f32[4,16,32,128]{3,2,1,0:T(8,128)} %bitcast.3), calls=%async_computation | async-start | bytes 2097152 | tf_op jit(solution)/shard_map/all_to_all | solution.py:35
  100.0 4.8 %collective-permute-start = (f32[16,3,128]{2,1,0:T(4,128)S(1)}, f32[16,3,128]{2,1,0:T(4,128)S(1)}, u32[]{:S(2)}, u32[]{:S(2)}) collective-permute-start(f32[16,3,128]{2,1,0:T(4,128)S(1)} %get-tuple-element.13), channel_id=1, source_target_pairs={{0,32},{32,64},{64,96},{1,33},{33,65},{65,97},{2,34},{34,66},{66,9... | collective-permute-start | bytes 73736 | tf_op jit(solution)/shard_map/ppermute | solution.py:19
  102.9 6.7 %collective-permute-start.1 = (f32[16,3,128]{2,1,0:T(4,128)S(1)}, f32[16,3,128]{2,1,0:T(4,128)S(1)}, u32[]{:S(2)}, u32[]{:S(2)}) collective-permute-start(f32[16,3,128]{2,1,0:T(4,128)S(1)} %get-tuple-element.14), channel_id=1, source_target_pairs={{32,0},{64,32},{96,64},{33,1},{65,33},{97,65},{34,2},{66,34},{98,6... | collective-permute-start | bytes 73736 | tf_op jit(solution)/shard_map/ppermute | solution.py:22
  109.6 2.7 %collective-permute-start.2 = (f32[3,38,128]{2,1,0:T(8,128)S(1)}, f32[3,38,128]{2,1,0:T(8,128)S(1)}, u32[]{:S(2)}, u32[]{:S(2)}) collective-permute-start(f32[3,38,128]{2,1,0:T(8,128)S(1)} %get-tuple-element.11), channel_id=1, source_target_pairs={{0,1},{1,2},{2,3},{3,4},{4,5},{5,6},{6,7},{7,8},{8,9},{9,10},{10,1... | collective-permute-start | bytes 175112 | tf_op jit(solution)/shard_map/ppermute | solution.py:19
  110.9 5.0 %collective-permute-start.3 = (f32[3,38,128]{2,1,0:T(8,128)S(1)}, f32[3,38,128]{2,1,0:T(8,128)S(1)}, u32[]{:S(2)}, u32[]{:S(2)}) collective-permute-start(f32[3,38,128]{2,1,0:T(8,128)S(1)} %get-tuple-element.12), channel_id=1, source_target_pairs={{1,0},{2,1},{3,2},{4,3},{5,4},{6,5},{7,6},{8,7},{9,8},{10,9},{11,1... | collective-permute-start | bytes 175112 | tf_op jit(solution)/shard_map/ppermute | solution.py:22

commit v2 on v1

v2 whole, which is shorter than its diff:
```python
import functools

import jax
import jax.numpy as jnp
from jax import lax
from jax.experimental import pallas as pl
from jax.experimental.pallas import tpu as pltpu
from jax.sharding import PartitionSpec as P

AXIAL = 0.35
CROSS = 0.06
PASSES = 3
MARGIN = 4
LATE_CHUNKS = 2
HELD_BACK = 4
MESH = pl.DeviceIdType.MESH


def diff_matrices(count):
    row = lax.broadcasted_iota(jnp.int32, (count, count), 0)
    col = lax.broadcasted_iota(jnp.int32, (count, count), 1)
    upper = (col == row + 1).astype(jnp.float32)
    lower = (col + 1 == row).astype(jnp.float32)
    along_rows = (upper - lower).astype(jnp.bfloat16)
    along_cols = (lower - upper).astype(jnp.bfloat16)
    return along_rows, along_cols


def strain_parts(field, x, diff_y, diff_z, low, high):
    center = [field[c, x] for c in range(3)]
    after = [field[c, x + 1].astype(jnp.float32) for c in range(3)]
    before = [field[c, x - 1].astype(jnp.float32) for c in range(3)]
    if high is not None:
        after = [value * high for value in after]
    if low is not None:
        before = [value * low for value in before]
    dx = [after[c] - before[c] for c in range(3)]
    dy = [jnp.dot(diff_y, center[c], preferred_element_type=jnp.float32) for c in range(3)]
    dz = [jnp.dot(center[c], diff_z, preferred_element_type=jnp.float32) for c in range(3)]
    return (dx[0], dy[1], dz[2], dx[1] + dy[0], dx[2] + dz[0], dy[2] + dz[1])


def pair_term(forward, adjoint, x, diff_y, diff_z, low=None, high=None):
    eu = strain_parts(forward, x, diff_y, diff_z, low, high)
    ev = strain_parts(adjoint, x, diff_y, diff_z, low, high)
    straight = eu[0] * ev[0] + eu[1] * ev[1] + eu[2] * ev[2]
    shear = eu[3] * ev[3] + eu[4] * ev[4] + eu[5] * ev[5]
    return straight + 0.5 * shear


def gradient_kernel(
    space,
    factor,
    modes,
    gains,
    out,
    buf,
    ymat,
    zmat,
    acc,
    rows_out,
    from_core,
    chip_sum,
    from_chip,
    from_side,
    grid0,
    grid1,
    grid2,
    load_sem,
    halo_sem,
    core_sem,
    chip_sem,
    side_sem,
):
    mode_count = modes.shape[1]
    planes = modes.shape[5]
    rows = modes.shape[6]
    cols = modes.shape[7]
    chunks = 2 * mode_count
    inner = planes - 2
    band = out.shape[1]
    block_rows = band + 2 * MARGIN
    me = lax.axis_index("space")
    freq = lax.axis_index("freq")
    core = lax.rem(freq, 2)
    chip = freq // 2
    other_core = freq + 1 - 2 * core
    other_chip = lax.rem(freq + 2, 4)
    above = lax.rem(me + 1, space)
    below = lax.rem(me + space - 1, space)

    def send(src, dst, sems, index, freq_to, space_to):
        return pltpu.make_async_remote_copy(
            src_ref=src,
            dst_ref=dst,
            send_sem=sems.at[(0, *index)],
            recv_sem=sems.at[(1, *index)],
            device_id={"freq": freq_to, "space": space_to},
            device_id_type=MESH,
        )

    def load(m):
        return pltpu.make_async_copy(
            modes.at[0, m], buf.at[m, :, :, :, pl.ds(1, planes)], load_sem.at[m]
        )

    def halo(c, side):
        m, part = c // 2, lax.rem(c, 2)
        plane, slot, target = (planes - 1, 0, above) if side == 0 else (0, planes + 1, below)
        return send(
            modes.at[0, m, :, part, :, plane],
            buf.at[m, :, part, :, slot],
            halo_sem,
            (side, c),
            freq,
            target,
        )

    def block(half, owner_core):
        start = pl.multiple_of((2 * half + owner_core) * band, 8)
        return pl.ds(start, block_rows)

    def to_core(late):
        first, count = (inner, 2) if late else (0, inner)
        return [
            send(
                rows_out.at[pl.ds(first, count), block(half, 1 - core)],
                from_core.at[half, pl.ds(first, count)],
                core_sem,
                (int(late), half),
                other_core,
                me,
            )
            for half in range(2)
        ]

    def to_chip(group):
        first, count = ((0, inner - HELD_BACK), (inner - HELD_BACK, HELD_BACK), (inner, 2))[group]
        return send(
            chip_sum.at[1 - chip, pl.ds(first, count)],
            from_chip.at[pl.ds(first, count)],
            chip_sem,
            (group,),
            other_chip,
            me,
        )

    def to_sides(late):
        spans = ((inner, 1, 2), (inner + 1, 1, 0)) if late else ((inner - 2, 2, 0), (0, 2, 1))
        copies = []
        for same in (1, 0):
            half, target_freq = (chip, freq) if same else (1 - chip, other_chip)
            for side, (first, count, slot) in enumerate(spans):
                copies.append(
                    send(
                        chip_sum.at[half, pl.ds(first, count)],
                        from_side.at[side, same, pl.ds(slot, count)],
                        side_sem,
                        (int(late), side, same),
                        target_freq,
                        above if side == 0 else below,
                    )
                )
        return copies

    def shift_rows(place):
        edge = jnp.zeros((MARGIN, cols), jnp.float32)
        rows_out[place] = jnp.concatenate([edge, acc[place], edge], axis=0)

    def add_cores(place):
        for half in range(2):
            chip_sum[half, place] = rows_out[place, block(half, core)] + from_core[half, place]

    load(0).start()
    barrier = pltpu.get_barrier_semaphore()
    for freq_to, space_to in (
        (freq, above),
        (freq, below),
        (other_core, me),
        (other_chip, me),
        (other_chip, above),
        (other_chip, below),
    ):
        pl.semaphore_signal(
            barrier, inc=1, device_id={"freq": freq_to, "space": space_to}, device_id_type=MESH
        )
    pl.semaphore_wait(barrier, 6)

    def start_halos(first, last):
        @pl.loop(first, last)
        def _(c):
            halo(c, 0).start()
            halo(c, 1).start()

    start_halos(0, chunks - LATE_CHUNKS)

    @pl.loop(1, mode_count)
    def _(m):
        load(m).start()

    diff_y, diff_z = diff_matrices(rows)
    ymat[...] = diff_y
    zmat[...] = diff_z
    acc[...] = jnp.zeros_like(acc)

    def term(m, part, x, low=None, high=None):
        return pair_term(
            buf.at[m, 0, part], buf.at[m, 1, part], x, ymat[...], zmat[...], low, high
        )

    @pl.loop(0, mode_count)
    def _(m):
        load(m).wait()
        weight = gains[0, m] * (0.25 * factor)

        @pl.loop(0, inner)
        def _(q):
            acc[q] += weight * (term(m, 0, q + 2) + term(m, 1, q + 2))

    @pl.loop(0, inner)
    def _(q):
        shift_rows(q)

    for copy in to_core(False):
        copy.start()
    for copy in to_core(False):
        copy.wait_recv()

    @pl.loop(0, inner)
    def _(q):
        add_cores(q)

    for copy in to_sides(False):
        copy.start()
    to_chip(0).start()
    start_halos(chunks - LATE_CHUNKS, chunks)
    to_chip(1).start()

    low = jnp.where(me > 0, 1.0, 0.0).astype(jnp.float32)
    high = jnp.where(me < space - 1, 1.0, 0.0).astype(jnp.float32)

    @pl.loop(0, chunks)
    def _(c):
        m, part = c // 2, lax.rem(c, 2)
        weight = gains[0, m] * (0.25 * factor)
        halo(c, 0).wait_recv()
        acc[inner + 1] += weight * term(m, part, 1, low=low)
        halo(c, 1).wait_recv()
        acc[inner] += weight * term(m, part, planes, high=high)

    shift_rows(inner)
    shift_rows(inner + 1)
    for copy in to_core(True):
        copy.start()
    for copy in to_core(True):
        copy.wait_recv()
    add_cores(inner)
    add_cores(inner + 1)
    to_chip(2).start()
    for copy in to_sides(True):
        copy.start()

    row = lax.broadcasted_iota(jnp.int32, (block_rows, cols), 0) + (freq * band - MARGIN)
    inside = ((row >= 0) & (row < rows)).astype(jnp.float32)
    col = lax.broadcasted_iota(jnp.int32, (block_rows, cols), 1)
    not_first = (col > 0).astype(jnp.float32)
    not_last = (col < cols - 1).astype(jnp.float32)

    def smoothed(source, i):
        center = source[i]
        axial = source[i + 1] + source[i - 1] - 2.0 * center
        cross = (
            pltpu.roll(center, 1, 0)
            + pltpu.roll(center, block_rows - 1, 0)
            + pltpu.roll(center, 1, 1) * not_first
            + pltpu.roll(center, cols - 1, 1) * not_last
            - 4.0 * center
        )
        return (center + AXIAL * axial + CROSS * cross) * inside

    def one_pass(step, first, last):
        source, target = ((grid0, grid1), (grid1, grid2), (grid2, None))[step]

        @pl.loop(first, last)
        def _(i):
            value = smoothed(source, i)
            if target is None:
                out[i - PASSES] = value[MARGIN : MARGIN + band]
            else:
                place = me * planes - PASSES + i
                kept = jnp.where((place >= 0) & (place < space * planes), 1.0, 0.0)
                target[i] = value * kept.astype(jnp.float32)

    to_chip(0).wait_recv()
    to_chip(1).wait_recv()

    @pl.loop(0, inner)
    def _(q):
        grid0[q + PASSES + 1] = chip_sum[chip, q] + from_chip[q]

    one_pass(0, PASSES + 2, PASSES + planes - 2)
    one_pass(1, PASSES + 3, PASSES + planes - 3)
    one_pass(2, PASSES + 4, PASSES + planes - 4)

    for copy in to_sides(False):
        copy.wait_recv()
    to_chip(2).wait_recv()
    for copy in to_sides(True):
        copy.wait_recv()
    grid0[PASSES + planes - 1] = chip_sum[chip, inner] + from_chip[inner]
    grid0[PASSES] = chip_sum[chip, inner + 1] + from_chip[inner + 1]
    for i in range(PASSES):
        grid0[i] = (from_side[0, 0, i] + from_side[0, 1, i]) * low
        grid0[PASSES + planes + i] = (from_side[1, 0, i] + from_side[1, 1, i]) * high
    for step in range(PASSES):
        one_pass(step, step + 1, PASSES + 2 + step)
        one_pass(step, PASSES + planes - 2 - step, 2 * PASSES + planes - 1 - step)

    @pl.loop(0, chunks)
    def _(c):
        halo(c, 0).wait_send()
        halo(c, 1).wait_send()

    for copy in (
        *to_core(False),
        *to_core(True),
        *(to_chip(group) for group in range(3)),
        *to_sides(False),
        *to_sides(True),
    ):
        copy.wait_send()


def local(saved_modes, mode_gains):
    freqs, mode_count, pair, parts, comps, planes, rows, cols = saved_modes.shape
    freq_total = freqs * lax.axis_size("freq")
    factor = -2.0 / (freq_total * mode_count)
    band = rows // freq_total
    block_rows = band + 2 * MARGIN
    padded_planes = planes + 2 * PASSES
    f32 = jnp.float32
    return pl.pallas_call(
        functools.partial(gradient_kernel, lax.axis_size("space"), factor),
        out_shape=jax.ShapeDtypeStruct((planes, band, cols), f32),
        in_specs=[
            pl.BlockSpec(memory_space=pl.ANY),
            pl.BlockSpec(memory_space=pltpu.SMEM),
        ],
        out_specs=pl.BlockSpec(memory_space=pltpu.VMEM),
        scratch_shapes=[
            pltpu.VMEM((mode_count, pair, parts, comps, planes + 2, rows, cols), jnp.bfloat16),
            pltpu.VMEM((rows, rows), jnp.bfloat16),
            pltpu.VMEM((cols, cols), jnp.bfloat16),
            pltpu.VMEM((planes, rows, cols), f32),
            pltpu.VMEM((planes, rows + 2 * MARGIN, cols), f32),
            pltpu.VMEM((2, planes, block_rows, cols), f32),
            pltpu.VMEM((2, planes, block_rows, cols), f32),
            pltpu.VMEM((planes, block_rows, cols), f32),
            pltpu.VMEM((2, 2, PASSES, block_rows, cols), f32),
            pltpu.VMEM((padded_planes, block_rows, cols), f32),
            pltpu.VMEM((padded_planes, block_rows, cols), f32),
            pltpu.VMEM((padded_planes, block_rows, cols), f32),
            pltpu.SemaphoreType.DMA((mode_count,)),
            pltpu.SemaphoreType.DMA((2, 2, 2 * mode_count)),
            pltpu.SemaphoreType.DMA((2, 2, 2)),
            pltpu.SemaphoreType.DMA((2, 3)),
            pltpu.SemaphoreType.DMA((2, 2, 2, 2)),
        ],
        compiler_params=pltpu.CompilerParams(
            collective_id=0, has_side_effects=True, vmem_limit_bytes=56 << 20
        ),
        name="gradient",
    )(saved_modes, mode_gains)


def solution(mesh):
    in_specs = (P("freq", None, None, None, None, "space", None, None), P("freq", None))
    out_specs = P("space", "freq", None)
    return jax.shard_map(local, mesh=mesh, in_specs=in_specs, out_specs=out_specs, check_vma=False)
```

time: 119 us -> 100 us (0.84)
  waiting for transfers between devices: 23.1 us -> 0 us
  Pallas kernels: 77 us -> 98.3 us
  starting transfers between devices: 12.9 us -> 0 us
  other arithmetic: 2.04 us -> 0 us
    pallas_call x1, Pallas kernels: 77 us -> 98.3 us  [local(): pl.pallas_call(functools.partial(gradient_kernel, lax.axis_size('space'),...]
    all_to_all x1 -> x0, waiting for transfers between devices: 14.8 us -> none  [sum_at_owner(): lax.all_to_all(tiles, axis, split_axis=0, concat_axis=0, tiled=True)]
    ppermute x4 -> x0, waiting for transfers between devices: 8.38 us -> none  [the longest x2 8.37 us: padded_2(): lax.ppermute(lax.slice_in_dim(block, 0, width, axis=dim), axis, backward)]
    ppermute x4 -> x0, starting transfers between devices: 7.38 us -> none  [the longest x2 4.17 us: padded_2(): lax.ppermute(lax.slice_in_dim(block, block.shape[dim] - width, None, axis...]
    all_to_all x1 -> x0, starting transfers between devices: 5.53 us -> none  [sum_at_owner(): lax.all_to_all(tiles, axis, split_axis=0, concat_axis=0, tiled=True)]
    reshape x1 -> x0, local copies, waits for them, and re-layouts: 2.34 us -> none  [split_up(): tiles = x.reshape(*dims[:dim], size, dims[dim] // size, *dims[dim + 1:])]
    unnamed x0 -> x1, local copies, waits for them, and re-layouts: none -> 1.67 us
    select_n x3 -> x0, other arithmetic: 1.61 us -> none  [deep_smooth(): jnp.where(valid_x[:, None, None] & valid_y[None, :, None], padded, 0.0)]
  transfers between devices with their start and end apart: 5 -> 0, of which waited for: 3 -> 0; matrix products, arithmetic and copies ran while one was open for 0% -> 0% of each run, Pallas kernels for 0% -> 0%
where the time goes in v2:
time: 100 us
  Pallas kernels  98.3 us (98%)
  local copies, waits for them, and re-layouts  1.67 us (2%)
    pallas_call x1, Pallas kernels, local(): pl.pallas_call(functools.partial(gradient_kernel, lax.axis_size('space'),...  98.3 us

profile of v2, /device:TPU:1, one launch (start us, length us, event | category | flops | bytes accessed | tf_op | source)
XLA Modules:
  0.0 100.0 jit_solution(9938916865064698975)
XLA Ops:
  0.0 98.3 %gradient.1 = f32[16,32,128]{2,1,0:T(8,128)} custom-call(bf16[1,4,2,2,3,16,128,128]{7,6,5,4,3,2,1,0:T(8,128)(2,1)} %modes.1, f32[1,4]{1,0:T(1,128)} %gains.1), custom_call_target="tpu_custom_call" | custom-call | tf_op jit(solution)/shard_map/gradient/pallas_call | solution.py:342
  98.3 1.7 %copy.4 = f32[16,32,128]{2,1,0:T(8,128)} copy(f32[16,32,128]{2,1,0:T(8,128)} %gradient.1) | data formatting | bytes 524288

commit v3 on v2

--- a/solution.py
+++ b/solution.py
@@ -26,23 +26,19 @@
     return along_rows, along_cols
 
 
-def strain_parts(field, x, diff_y, diff_z, low, high):
+def strain_parts(field, x, diff_y, diff_z):
     center = [field[c, x] for c in range(3)]
     after = [field[c, x + 1].astype(jnp.float32) for c in range(3)]
     before = [field[c, x - 1].astype(jnp.float32) for c in range(3)]
-    if high is not None:
-        after = [value * high for value in after]
-    if low is not None:
-        before = [value * low for value in before]
     dx = [after[c] - before[c] for c in range(3)]
     dy = [jnp.dot(diff_y, center[c], preferred_element_type=jnp.float32) for c in range(3)]
     dz = [jnp.dot(center[c], diff_z, preferred_element_type=jnp.float32) for c in range(3)]
     return (dx[0], dy[1], dz[2], dx[1] + dy[0], dx[2] + dz[0], dy[2] + dz[1])
 
 
-def pair_term(forward, adjoint, x, diff_y, diff_z, low=None, high=None):
-    eu = strain_parts(forward, x, diff_y, diff_z, low, high)
-    ev = strain_parts(adjoint, x, diff_y, diff_z, low, high)
+def pair_term(forward, adjoint, x, diff_y, diff_z):
+    eu = strain_parts(forward, x, diff_y, diff_z)
+    ev = strain_parts(adjoint, x, diff_y, diff_z)
     straight = eu[0] * ev[0] + eu[1] * ev[1] + eu[2] * ev[2]
     shear = eu[3] * ev[3] + eu[4] * ev[4] + eu[5] * ev[5]
     return straight + 0.5 * shear
@@ -86,8 +82,12 @@
     chip = freq // 2
     other_core = freq + 1 - 2 * core
     other_chip = lax.rem(freq + 2, 4)
-    above = lax.rem(me + 1, space)
-    below = lax.rem(me + space - 1, space)
+    far = 1 - lax.rem(me, 2)
+    near = 1 - far
+    has_far = (me > 0) & (me < space - 1)
+
+    def slab(side):
+        return lax.rem(me + 1 - 2 * side + space, space)
 
     def send(src, dst, sems, index, freq_to, space_to):
         return pltpu.make_async_remote_copy(
@@ -106,36 +106,33 @@
 
     def halo(c, side):
         m, part = c // 2, lax.rem(c, 2)
-        plane, slot, target = (planes - 1, 0, above) if side == 0 else (0, planes + 1, below)
         return send(
-            modes.at[0, m, :, part, :, plane],
-            buf.at[m, :, part, :, slot],
+            modes.at[0, m, :, part, :, (planes - 1) * (1 - side)],
+            buf.at[m, :, part, :, (planes + 1) * side],
             halo_sem,
             (side, c),
             freq,
-            target,
+            slab(side),
         )
 
     def block(half, owner_core):
         start = pl.multiple_of((2 * half + owner_core) * band, 8)
         return pl.ds(start, block_rows)
 
-    def to_core(late):
-        first, count = (inner, 2) if late else (0, inner)
+    def to_core(stage, first, count):
         return [
             send(
                 rows_out.at[pl.ds(first, count), block(half, 1 - core)],
                 from_core.at[half, pl.ds(first, count)],
                 core_sem,
-                (int(late), half),
+                (stage, half),
                 other_core,
                 me,
             )
             for half in range(2)
         ]
 
-    def to_chip(group):
-        first, count = ((0, inner - HELD_BACK), (inner - HELD_BACK, HELD_BACK), (inner, 2))[group]
+    def to_chip(group, first, count):
         return send(
             chip_sum.at[1 - chip, pl.ds(first, count)],
             from_chip.at[pl.ds(first, count)],
@@ -145,23 +142,23 @@
             me,
         )
 
-    def to_sides(late):
-        spans = ((inner, 1, 2), (inner + 1, 1, 0)) if late else ((inner - 2, 2, 0), (0, 2, 1))
-        copies = []
-        for same in (1, 0):
-            half, target_freq = (chip, freq) if same else (1 - chip, other_chip)
-            for side, (first, count, slot) in enumerate(spans):
-                copies.append(
-                    send(
-                        chip_sum.at[half, pl.ds(first, count)],
-                        from_side.at[side, same, pl.ds(slot, count)],
-                        side_sem,
-                        (int(late), side, same),
-                        target_freq,
-                        above if side == 0 else below,
-                    )
-                )
-        return copies
+    def to_side(side, late, same):
+        if late:
+            first, count, slot = inner + side, 1, 2 - 2 * side
+        else:
+            first, count, slot = (inner - 2) * (1 - side), 2, side
+        half, target_freq = (chip, freq) if same else (1 - chip, other_chip)
+        return send(
+            chip_sum.at[half, pl.ds(first, count)],
+            from_side.at[side, same, pl.ds(slot, count)],
+            side_sem,
+            (side, int(late), same),
+            target_freq,
+            slab(side),
+        )
+
+    def bulk(group):
+        return to_chip(group, *((0, inner - HELD_BACK), (inner - HELD_BACK, HELD_BACK))[group])
 
     def shift_rows(place):
         edge = jnp.zeros((MARGIN, cols), jnp.float32)
@@ -173,24 +170,31 @@
 
     load(0).start()
     barrier = pltpu.get_barrier_semaphore()
-    for freq_to, space_to in (
-        (freq, above),
-        (freq, below),
-        (other_core, me),
-        (other_chip, me),
-        (other_chip, above),
-        (other_chip, below),
-    ):
+
+    def greet(freq_to, space_to):
         pl.semaphore_signal(
             barrier, inc=1, device_id={"freq": freq_to, "space": space_to}, device_id_type=MESH
         )
-    pl.semaphore_wait(barrier, 6)
+
+    @pl.when(has_far)
+    def _():
+        greet(freq, slab(far))
+        greet(other_chip, slab(far))
+
+    greet(freq, slab(near))
+    greet(other_chip, slab(near))
+    greet(other_chip, me)
+    greet(other_core, me)
+    pl.semaphore_wait(barrier, jnp.where(has_far, 6, 4))
 
     def start_halos(first, last):
         @pl.loop(first, last)
         def _(c):
-            halo(c, 0).start()
-            halo(c, 1).start()
+            @pl.when(has_far)
+            def _():
+                halo(c, far).start()
+
+            halo(c, near).start()
 
     start_halos(0, chunks - LATE_CHUNKS)
 
@@ -203,10 +207,18 @@
     zmat[...] = diff_z
     acc[...] = jnp.zeros_like(acc)
 
-    def term(m, part, x, low=None, high=None):
-        return pair_term(
-            buf.at[m, 0, part], buf.at[m, 1, part], x, ymat[...], zmat[...], low, high
-        )
+    @pl.when(jnp.logical_not(has_far))
+    def _():
+        @pl.loop(0, mode_count)
+        def _(m):
+            outer = buf.at[m, :, :, :, (planes + 1) * (1 - far)]
+            outer[...] = jnp.zeros(outer.shape, outer.dtype)
+
+        missing = from_side.at[1 - far]
+        missing[...] = jnp.zeros(missing.shape, missing.dtype)
+
+    def term(m, part, x):
+        return pair_term(buf.at[m, 0, part], buf.at[m, 1, part], x, ymat[...], zmat[...])
 
     @pl.loop(0, mode_count)
     def _(m):
@@ -221,44 +233,70 @@
     def _(q):
         shift_rows(q)
 
-    for copy in to_core(False):
+    early = to_core(0, 0, inner)
+    for copy in early:
         copy.start()
-    for copy in to_core(False):
+    for copy in early:
         copy.wait_recv()
 
     @pl.loop(0, inner)
     def _(q):
         add_cores(q)
 
-    for copy in to_sides(False):
+    @pl.when(has_far)
+    def _():
+        for same in (1, 0):
+            to_side(far, False, same).start()
+
+    for same in (1, 0):
+        to_side(near, False, same).start()
+    bulk(0).start()
+    start_halos(chunks - LATE_CHUNKS, chunks)
+    bulk(1).start()
+
+    far_place = inner + far
+    near_place = inner + near
+
+    def late_core(stage):
+        return to_core(stage, far_place if stage == 1 else near_place, 1)
+
+    @pl.loop(0, 2 * chunks)
+    def _(i):
+        c, side = i // 2, lax.rem(i + far, 2)
+        m, part = c // 2, lax.rem(c, 2)
+
+        @pl.when((side == near) | has_far)
+        def _():
+            halo(c, 1 - side).wait_recv()
+
+        weight = gains[0, m] * (0.25 * factor)
+        acc[inner + side] += weight * term(m, part, planes - (planes - 1) * side)
+
+        @pl.when(i == 2 * chunks - 2)
+        def _():
+            shift_rows(far_place)
+            for copy in late_core(1):
+                copy.start()
+
+    shift_rows(near_place)
+    for copy in late_core(2):
         copy.start()
-    to_chip(0).start()
-    start_halos(chunks - LATE_CHUNKS, chunks)
-    to_chip(1).start()
-
-    low = jnp.where(me > 0, 1.0, 0.0).astype(jnp.float32)
-    high = jnp.where(me < space - 1, 1.0, 0.0).astype(jnp.float32)
-
-    @pl.loop(0, chunks)
-    def _(c):
-        m, part = c // 2, lax.rem(c, 2)
-        weight = gains[0, m] * (0.25 * factor)
-        halo(c, 0).wait_recv()
-        acc[inner + 1] += weight * term(m, part, 1, low=low)
-        halo(c, 1).wait_recv()
-        acc[inner] += weight * term(m, part, planes, high=high)
-
-    shift_rows(inner)
-    shift_rows(inner + 1)
-    for copy in to_core(True):
-        copy.start()
-    for copy in to_core(True):
+    for copy in late_core(1):
         copy.wait_recv()
-    add_cores(inner)
-    add_cores(inner + 1)
-    to_chip(2).start()
-    for copy in to_sides(True):
-        copy.start()
+    add_cores(far_place)
+
+    @pl.when(has_far)
+    def _():
+        for same in (1, 0):
+            to_side(far, True, same).start()
+
+    to_chip(2, far_place, 1).start()
+    for copy in late_core(2):
+        copy.wait_recv()
+    add_cores(near_place)
+    to_chip(3, near_place, 1).start()
+    for same in (1, 0):
+        to_side(near, True, same).start()
 
     row = lax.broadcasted_iota(jnp.int32, (block_rows, cols), 0) + (freq * band - MARGIN)
     inside = ((row >= 0) & (row < rows)).astype(jnp.float32)
@@ -291,8 +329,8 @@
                 kept = jnp.where((place >= 0) & (place < space * planes), 1.0, 0.0)
                 target[i] = value * kept.astype(jnp.float32)
 
-    to_chip(0).wait_recv()
-    to_chip(1).wait_recv()
+    bulk(0).wait_recv()
+    bulk(1).wait_recv()
 
     @pl.loop(0, inner)
     def _(q):
@@ -302,31 +340,51 @@
     one_pass(1, PASSES + 3, PASSES + planes - 3)
     one_pass(2, PASSES + 4, PASSES + planes - 4)
 
-    for copy in to_sides(False):
-        copy.wait_recv()
-    to_chip(2).wait_recv()
-    for copy in to_sides(True):
-        copy.wait_recv()
+    def wait_sides(late):
+        @pl.when(has_far)
+        def _():
+            for same in (1, 0):
+                to_side(1 - far, late, same).wait_recv()
+
+        for same in (1, 0):
+            to_side(1 - near, late, same).wait_recv()
+
+    wait_sides(False)
+    to_chip(2, far_place, 1).wait_recv()
+    to_chip(3, near_place, 1).wait_recv()
+    wait_sides(True)
     grid0[PASSES + planes - 1] = chip_sum[chip, inner] + from_chip[inner]
     grid0[PASSES] = chip_sum[chip, inner + 1] + from_chip[inner + 1]
     for i in range(PASSES):
-        grid0[i] = (from_side[0, 0, i] + from_side[0, 1, i]) * low
-        grid0[PASSES + planes + i] = (from_side[1, 0, i] + from_side[1, 1, i]) * high
+        grid0[i] = from_side[0, 0, i] + from_side[0, 1, i]
+        grid0[PASSES + planes + i] = from_side[1, 0, i] + from_side[1, 1, i]
     for step in range(PASSES):
         one_pass(step, step + 1, PASSES + 2 + step)
         one_pass(step, PASSES + planes - 2 - step, 2 * PASSES + planes - 1 - step)
 
     @pl.loop(0, chunks)
     def _(c):
-        halo(c, 0).wait_send()
-        halo(c, 1).wait_send()
+        @pl.when(has_far)
+        def _():
+            halo(c, far).wait_send()
+
+        halo(c, near).wait_send()
+
+    @pl.when(has_far)
+    def _():
+        for late in (False, True):
+            for same in (1, 0):
+                to_side(far, late, same).wait_send()
 
     for copy in (
-        *to_core(False),
-        *to_core(True),
-        *(to_chip(group) for group in range(3)),
-        *to_sides(False),
-        *to_sides(True),
+        *early,
+        *late_core(1),
+        *late_core(2),
+        bulk(0),
+        bulk(1),
+        to_chip(2, far_place, 1),
+        to_chip(3, near_place, 1),
+        *(to_side(near, late, same) for late in (False, True) for same in (1, 0)),
     ):
         copy.wait_send()
 
@@ -362,12 +420,12 @@
             pltpu.VMEM((padded_planes, block_rows, cols), f32),
             pltpu.SemaphoreType.DMA((mode_count,)),
             pltpu.SemaphoreType.DMA((2, 2, 2 * mode_count)),
-            pltpu.SemaphoreType.DMA((2, 2, 2)),
-            pltpu.SemaphoreType.DMA((2, 3)),
+            pltpu.SemaphoreType.DMA((2, 3, 2)),
+            pltpu.SemaphoreType.DMA((2, 4)),
             pltpu.SemaphoreType.DMA((2, 2, 2, 2)),
         ],
         compiler_params=pltpu.CompilerParams(
-            collective_id=0, has_side_effects=True, vmem_limit_bytes=56 << 20
+            collective_id=0, has_side_effects=True, vmem_limit_bytes=40 << 20
         ),
         name="gradient",
     )(saved_modes, mode_gains)

time: 100 us -> 90.6 us (0.906); the launches traced: 100 us -> 89.5 us
  Pallas kernels: 98.3 us -> 88.1 us
    pallas_call x1, Pallas kernels: 98.3 us -> 88.1 us  [local(): pl.pallas_call(functools.partial(gradient_kernel, lax.axis_size('space'),...]
where the time goes in v3:
time: 90.6 us; the launch traced here: 89.5 us
  Pallas kernels  88.1 us (97%)
  local copies, waits for them, and re-layouts  1.36 us (2%)
    pallas_call x1, Pallas kernels, local(): pl.pallas_call(functools.partial(gradient_kernel, lax.axis_size('space'),...  88.1 us

profile of v3, /device:TPU:1, one launch (start us, length us, event | category | flops | bytes accessed | tf_op | source)
XLA Modules:
  0.0 89.5 jit_solution(15966762405791960167)
XLA Ops:
  0.0 0.0 copy-start
  0.0 0.7 copy-done
  0.7 88.1 %gradient.1 = f32[16,32,128]{2,1,0:T(8,128)S(1)} custom-call(bf16[1,4,2,2,3,16,128,128]{7,6,5,4,3,2,1,0:T(8,128)(2,1)} %modes.1, f32[1,4]{1,0:T(1,128)S(1)} %copy-done), custom_call_target="tpu_custom_call" | custom-call | tf_op jit(solution)/shard_map/gradient/pallas_call | solution.py:400
  88.8 0.7 copy.4
Async XLA Ops:
  0.0 0.7 copy-start

commit v4 on v3

--- a/solution.py
+++ b/solution.py
@@ -12,7 +12,7 @@
 PASSES = 3
 MARGIN = 4
 LATE_CHUNKS = 2
-HELD_BACK = 4
+HELD_BACK = 6
 MESH = pl.DeviceIdType.MESH
 
 
@@ -57,11 +57,17 @@
     rows_out,
     from_core,
     chip_sum,
+    smooth_sum,
     from_chip,
+    late_chip,
     from_side,
+    late_side,
     grid0,
     grid1,
     grid2,
+    late0,
+    late1,
+    late2,
     load_sem,
     halo_sem,
     core_sem,
@@ -132,9 +138,11 @@
             for half in range(2)
         ]
 
-    def to_chip(group, first, count):
+    def bulk(group):
+        split = planes - HELD_BACK
+        first, count = ((0, split), (split, HELD_BACK))[group]
         return send(
-            chip_sum.at[1 - chip, pl.ds(first, count)],
+            smooth_sum.at[pl.ds(first, count)],
             from_chip.at[pl.ds(first, count)],
             chip_sem,
             (group,),
@@ -142,23 +150,36 @@
             me,
         )
 
-    def to_side(side, late, same):
-        if late:
-            first, count, slot = inner + side, 1, 2 - 2 * side
-        else:
-            first, count, slot = (inner - 2) * (1 - side), 2, side
+    def late_to_chip(side):
+        return send(
+            chip_sum.at[1 - chip, inner + side],
+            late_chip.at[side],
+            chip_sem,
+            (2 + side,),
+            other_chip,
+            me,
+        )
+
+    def early_to_side(side, half):
+        return send(
+            chip_sum.at[half, pl.ds((inner - 2) * (1 - side), 2)],
+            from_side.at[side, half],
+            side_sem,
+            (side, half),
+            other_chip,
+            slab(side),
+        )
+
+    def late_to_side(side, same):
         half, target_freq = (chip, freq) if same else (1 - chip, other_chip)
         return send(
-            chip_sum.at[half, pl.ds(first, count)],
-            from_side.at[side, same, pl.ds(slot, count)],
+            chip_sum.at[half, inner + side],
+            late_side.at[side, same],
             side_sem,
-            (side, int(late), same),
+            (side, 2 + same),
             target_freq,
             slab(side),
         )
-
-    def bulk(group):
-        return to_chip(group, *((0, inner - HELD_BACK), (inner - HELD_BACK, HELD_BACK))[group])
 
     def shift_rows(place):
         edge = jnp.zeros((MARGIN, cols), jnp.float32)
@@ -214,8 +235,9 @@
             outer = buf.at[m, :, :, :, (planes + 1) * (1 - far)]
             outer[...] = jnp.zeros(outer.shape, outer.dtype)
 
-        missing = from_side.at[1 - far]
-        missing[...] = jnp.zeros(missing.shape, missing.dtype)
+        for landing in (from_side, late_side):
+            missing = landing.at[1 - far]
+            missing[...] = jnp.zeros(missing.shape, missing.dtype)
 
     def term(m, part, x):
         return pair_term(buf.at[m, 0, part], buf.at[m, 1, part], x, ymat[...], zmat[...])
@@ -245,61 +267,13 @@
 
     @pl.when(has_far)
     def _():
-        for same in (1, 0):
-            to_side(far, False, same).start()
-
-    for same in (1, 0):
-        to_side(near, False, same).start()
-    bulk(0).start()
-    start_halos(chunks - LATE_CHUNKS, chunks)
-    bulk(1).start()
-
-    far_place = inner + far
-    near_place = inner + near
-
-    def late_core(stage):
-        return to_core(stage, far_place if stage == 1 else near_place, 1)
-
-    @pl.loop(0, 2 * chunks)
-    def _(i):
-        c, side = i // 2, lax.rem(i + far, 2)
-        m, part = c // 2, lax.rem(c, 2)
-
-        @pl.when((side == near) | has_far)
-        def _():
-            halo(c, 1 - side).wait_recv()
-
-        weight = gains[0, m] * (0.25 * factor)
-        acc[inner + side] += weight * term(m, part, planes - (planes - 1) * side)
-
-        @pl.when(i == 2 * chunks - 2)
-        def _():
-            shift_rows(far_place)
-            for copy in late_core(1):
-                copy.start()
-
-    shift_rows(near_place)
-    for copy in late_core(2):
-        copy.start()
-    for copy in late_core(1):
-        copy.wait_recv()
-    add_cores(far_place)
-
-    @pl.when(has_far)
-    def _():
-        for same in (1, 0):
-            to_side(far, True, same).start()
-
-    to_chip(2, far_place, 1).start()
-    for copy in late_core(2):
-        copy.wait_recv()
-    add_cores(near_place)
-    to_chip(3, near_place, 1).start()
-    for same in (1, 0):
-        to_side(near, True, same).start()
-
-    row = lax.broadcasted_iota(jnp.int32, (block_rows, cols), 0) + (freq * band - MARGIN)
-    inside = ((row >= 0) & (row < rows)).astype(jnp.float32)
+        for half in range(2):
+            early_to_side(far, half).start()
+
+    for half in range(2):
+        early_to_side(near, half).start()
+
+    row = lax.broadcasted_iota(jnp.int32, (block_rows, cols), 0) - MARGIN
     col = lax.broadcasted_iota(jnp.int32, (block_rows, cols), 1)
     not_first = (col > 0).astype(jnp.float32)
     not_last = (col < cols - 1).astype(jnp.float32)
@@ -314,53 +288,137 @@
             + pltpu.roll(center, cols - 1, 1) * not_last
             - 4.0 * center
         )
-        return (center + AXIAL * axial + CROSS * cross) * inside
-
-    def one_pass(step, first, last):
-        source, target = ((grid0, grid1), (grid1, grid2), (grid2, None))[step]
-
-        @pl.loop(first, last)
-        def _(i):
-            value = smoothed(source, i)
-            if target is None:
-                out[i - PASSES] = value[MARGIN : MARGIN + band]
-            else:
+        return center + AXIAL * axial + CROSS * cross
+
+    def one_pass(source, target, half, first, count, width):
+        at_row = row + (2 * half + core) * band
+        inside = ((at_row >= 0) & (at_row < rows)).astype(jnp.float32)
+
+        @pl.loop(0, count // width)
+        def _(k):
+            for j in range(width):
+                i = first + k * width + j
                 place = me * planes - PASSES + i
                 kept = jnp.where((place >= 0) & (place < space * planes), 1.0, 0.0)
-                target[i] = value * kept.astype(jnp.float32)
+                target[i] = smoothed(source, i) * (inside * kept.astype(jnp.float32))
+
+    def last_pass(source, first, count, width, store):
+        @pl.loop(0, count // width)
+        def _(k):
+            for j in range(width):
+                i = first + k * width + j
+                store(i - PASSES, smoothed(source, i)[MARGIN : MARGIN + band])
+
+    def smooth_early(half, store):
+        @pl.loop(0, inner)
+        def _(q):
+            grid0[q + PASSES + 1] = chip_sum[half, q]
+
+        for i in range(2):
+            grid0[i] = from_side[0, half, i]
+            grid0[PASSES + planes + 1 + i] = from_side[1, half, i]
+        one_pass(grid0, grid1, half, 1, planes + 4, 2)
+        one_pass(grid1, grid2, half, 2, planes + 2, 2)
+        last_pass(grid2, 3, planes, 2, store)
+
+    def keep(p, value):
+        out[p] = value
+
+    def pass_on(p, value):
+        smooth_sum[p] = value
+
+    for edge in (grid0, late0, late1, late2):
+        edge[...] = jnp.zeros_like(edge)
+
+    @pl.when(has_far)
+    def _():
+        for half in range(2):
+            early_to_side(1 - far, half).wait_recv()
+
+    for half in range(2):
+        early_to_side(1 - near, half).wait_recv()
+    smooth_early(1 - chip, pass_on)
+    bulk(0).start()
+    start_halos(chunks - LATE_CHUNKS, chunks)
+    bulk(1).start()
+    smooth_early(chip, keep)
+
+    far_place = inner + far
+    near_place = inner + near
+
+    def late_core(stage):
+        return to_core(stage, far_place if stage == 1 else near_place, 1)
+
+    @pl.loop(0, 2 * chunks)
+    def _(i):
+        c, side = i // 2, lax.rem(i + far, 2)
+        m, part = c // 2, lax.rem(c, 2)
+
+        @pl.when((side == near) | has_far)
+        def _():
+            halo(c, 1 - side).wait_recv()
+
+        weight = gains[0, m] * (0.25 * factor)
+        acc[inner + side] += weight * term(m, part, planes - (planes - 1) * side)
+
+        @pl.when(i == 2 * chunks - 2)
+        def _():
+            shift_rows(far_place)
+            for copy in late_core(1):
+                copy.start()
+
+    shift_rows(near_place)
+    for copy in late_core(2):
+        copy.start()
+    for copy in late_core(1):
+        copy.wait_recv()
+    add_cores(far_place)
+
+    @pl.when(has_far)
+    def _():
+        for same in (1, 0):
+            late_to_side(far, same).start()
+
+    late_to_chip(far).start()
+    for copy in late_core(2):
+        copy.wait_recv()
+    add_cores(near_place)
+    late_to_chip(near).start()
+    for same in (1, 0):
+        late_to_side(near, same).start()
 
     bulk(0).wait_recv()
     bulk(1).wait_recv()
 
-    @pl.loop(0, inner)
-    def _(q):
-        grid0[q + PASSES + 1] = chip_sum[chip, q] + from_chip[q]
-
-    one_pass(0, PASSES + 2, PASSES + planes - 2)
-    one_pass(1, PASSES + 3, PASSES + planes - 3)
-    one_pass(2, PASSES + 4, PASSES + planes - 4)
-
-    def wait_sides(late):
-        @pl.when(has_far)
-        def _():
-            for same in (1, 0):
-                to_side(1 - far, late, same).wait_recv()
-
+    @pl.loop(0, planes)
+    def _(p):
+        out[p] += from_chip[p]
+
+    def add_late(p, value):
+        out[p] += value
+
+    def smooth_late(side):
+        late0[PASSES + (planes - 1) * (1 - side)] = chip_sum[chip, inner + side] + late_chip[side]
+        late0[PASSES - 1 + (planes + 1) * (1 - side)] = (
+            late_side[1 - side, 0] + late_side[1 - side, 1]
+        )
+        start = [(planes + 1 - step) * (1 - side) + (1 + step) * side for step in range(PASSES)]
+        one_pass(late0, late1, chip, start[0], 4, 4)
+        one_pass(late1, late2, chip, start[1], 4, 4)
+        last_pass(late2, start[2], 4, 4, add_late)
+
+    late_to_chip(far).wait_recv()
+
+    @pl.when(has_far)
+    def _():
         for same in (1, 0):
-            to_side(1 - near, late, same).wait_recv()
-
-    wait_sides(False)
-    to_chip(2, far_place, 1).wait_recv()
-    to_chip(3, near_place, 1).wait_recv()
-    wait_sides(True)
-    grid0[PASSES + planes - 1] = chip_sum[chip, inner] + from_chip[inner]
-    grid0[PASSES] = chip_sum[chip, inner + 1] + from_chip[inner + 1]
-    for i in range(PASSES):
-        grid0[i] = from_side[0, 0, i] + from_side[0, 1, i]
-        grid0[PASSES + planes + i] = from_side[1, 0, i] + from_side[1, 1, i]
-    for step in range(PASSES):
-        one_pass(step, step + 1, PASSES + 2 + step)
-        one_pass(step, PASSES + planes - 2 - step, 2 * PASSES + planes - 1 - step)
+            late_to_side(1 - far, same).wait_recv()
+
+    smooth_late(far)
+    late_to_chip(near).wait_recv()
+    for same in (1, 0):
+        late_to_side(1 - near, same).wait_recv()
+    smooth_late(near)
 
     @pl.loop(0, chunks)
     def _(c):
@@ -370,11 +428,16 @@
 
         halo(c, near).wait_send()
 
+    def to_side(side):
+        return (
+            *(early_to_side(side, half) for half in range(2)),
+            *(late_to_side(side, same) for same in (1, 0)),
+        )
+
     @pl.when(has_far)
     def _():
-        for late in (False, True):
-            for same in (1, 0):
-                to_side(far, late, same).wait_send()
+        for copy in to_side(far):
+            copy.wait_send()
 
     for copy in (
         *early,
@@ -382,9 +445,9 @@
         *late_core(2),
         bulk(0),
         bulk(1),
-        to_chip(2, far_place, 1),
-        to_chip(3, near_place, 1),
-        *(to_side(near, late, same) for late in (False, True) for same in (1, 0)),
+        late_to_chip(far),
+        late_to_chip(near),
+        *to_side(near),
     ):
         copy.wait_send()
 
@@ -413,8 +476,14 @@
             pltpu.VMEM((planes, rows + 2 * MARGIN, cols), f32),
             pltpu.VMEM((2, planes, block_rows, cols), f32),
             pltpu.VMEM((2, planes, block_rows, cols), f32),
-            pltpu.VMEM((planes, block_rows, cols), f32),
-            pltpu.VMEM((2, 2, PASSES, block_rows, cols), f32),
+            pltpu.VMEM((planes, band, cols), f32),
+            pltpu.VMEM((planes, band, cols), f32),
+            pltpu.VMEM((2, block_rows, cols), f32),
+            pltpu.VMEM((2, 2, 2, block_rows, cols), f32),
+            pltpu.VMEM((2, 2, block_rows, cols), f32),
+            pltpu.VMEM((padded_planes, block_rows, cols), f32),
+            pltpu.VMEM((padded_planes, block_rows, cols), f32),
+            pltpu.VMEM((padded_planes, block_rows, cols), f32),
             pltpu.VMEM((padded_planes, block_rows, cols), f32),
             pltpu.VMEM((padded_planes, block_rows, cols), f32),
             pltpu.VMEM((padded_planes, block_rows, cols), f32),
@@ -422,7 +491,7 @@
             pltpu.SemaphoreType.DMA((2, 2, 2 * mode_count)),
             pltpu.SemaphoreType.DMA((2, 3, 2)),
             pltpu.SemaphoreType.DMA((2, 4)),
-            pltpu.SemaphoreType.DMA((2, 2, 2, 2)),
+            pltpu.SemaphoreType.DMA((2, 2, 4)),
         ],
         compiler_params=pltpu.CompilerParams(
             collective_id=0, has_side_effects=True, vmem_limit_bytes=40 << 20

time: 90.6 us -> 86.7 us (0.957)
  Pallas kernels: 88.1 us -> 84.6 us
    pallas_call x1, Pallas kernels: 88.1 us -> 84.6 us  [local(): pl.pallas_call(functools.partial(gradient_kernel, lax.axis_size('space'),...]
where the time goes in v4:
time: 86.7 us; the launch traced here: 86 us
  Pallas kernels  84.6 us (98%)
  local copies, waits for them, and re-layouts  1.36 us (2%)
    pallas_call x1, Pallas kernels, local(): pl.pallas_call(functools.partial(gradient_kernel, lax.axis_size('space'),...  84.6 us

profile of v4, /device:TPU:1, one launch (start us, length us, event | category | flops | bytes accessed | tf_op | source)
XLA Modules:
  0.0 86.0 jit_solution(15172704862115338194)
XLA Ops:
  0.0 0.0 copy-start
  0.0 0.7 copy-done
  0.7 84.6 %gradient.1 = f32[16,32,128]{2,1,0:T(8,128)S(1)} custom-call(bf16[1,4,2,2,3,16,128,128]{7,6,5,4,3,2,1,0:T(8,128)(2,1)} %modes.1, f32[1,4]{1,0:T(1,128)S(1)} %copy-done), custom_call_target="tpu_custom_call" | custom-call | tf_op jit(solution)/shard_map/gradient/pallas_call | solution.py:463
  85.3 0.7 copy.4
Async XLA Ops:
  0.0 0.7 copy-start

commit v5 on v4

--- a/solution.py
+++ b/solution.py
@@ -12,7 +12,7 @@
 PASSES = 3
 MARGIN = 4
 LATE_CHUNKS = 2
-HELD_BACK = 6
+HELD_BACK = 10
 MESH = pl.DeviceIdType.MESH
 
 
@@ -73,6 +73,8 @@
     core_sem,
     chip_sem,
     side_sem,
+    core_in,
+    chip_in,
 ):
     mode_count = modes.shape[1]
     planes = modes.shape[5]
@@ -200,13 +202,18 @@
     @pl.when(has_far)
     def _():
         greet(freq, slab(far))
-        greet(other_chip, slab(far))
 
     greet(freq, slab(near))
-    greet(other_chip, slab(near))
-    greet(other_chip, me)
-    greet(other_core, me)
-    pl.semaphore_wait(barrier, jnp.where(has_far, 6, 4))
+
+    @pl.when(core == 0)
+    def _():
+        greet(other_core, me)
+
+    @pl.when(chip == 0)
+    def _():
+        greet(other_chip, me)
+
+    pl.semaphore_wait(barrier, jnp.where(has_far, 2, 1) + core + chip)
 
     def start_halos(first, last):
         @pl.loop(first, last)
@@ -219,6 +226,19 @@
 
     start_halos(0, chunks - LATE_CHUNKS)
 
+    def answer(sem, freq_to):
+        pl.semaphore_signal(
+            sem, inc=1, device_id={"freq": freq_to, "space": me}, device_id_type=MESH
+        )
+
+    @pl.when(core == 1)
+    def _():
+        answer(core_in, other_core)
+
+    @pl.when(chip == 1)
+    def _():
+        answer(chip_in, other_chip)
+
     @pl.loop(1, mode_count)
     def _(m):
         load(m).start()
@@ -254,6 +274,15 @@
     @pl.loop(0, inner)
     def _(q):
         shift_rows(q)
+
+    @pl.when(core == 0)
+    def _():
+        pl.semaphore_wait(core_in, 1)
+
+    @pl.when(chip == 0)
+    def _():
+        pl.semaphore_wait(chip_in, 1)
+        answer(chip_in, other_chip)
 
     early = to_core(0, 0, inner)
     for copy in early:
@@ -264,6 +293,10 @@
     @pl.loop(0, inner)
     def _(q):
         add_cores(q)
+
+    @pl.when(chip == 1)
+    def _():
+        pl.semaphore_wait(chip_in, 1)
 
     @pl.when(has_far)
     def _():
@@ -492,6 +525,8 @@
             pltpu.SemaphoreType.DMA((2, 3, 2)),
             pltpu.SemaphoreType.DMA((2, 4)),
             pltpu.SemaphoreType.DMA((2, 2, 4)),
+            pltpu.SemaphoreType.REGULAR,
+            pltpu.SemaphoreType.REGULAR,
         ],
         compiler_params=pltpu.CompilerParams(
             collective_id=0, has_side_effects=True, vmem_limit_bytes=40 << 20

time: 86.7 us -> 85.8 us (0.990)
  Pallas kernels: 84.6 us -> 83.3 us
    pallas_call x1, Pallas kernels: 84.6 us -> 83.3 us  [local(): pl.pallas_call(functools.partial(gradient_kernel, lax.axis_size('space'),...]
where the time goes in v5:
time: 85.8 us; the launch traced here: 84.7 us
  Pallas kernels  83.3 us (97%)
  local copies, waits for them, and re-layouts  1.36 us (2%)
    pallas_call x1, Pallas kernels, local(): pl.pallas_call(functools.partial(gradient_kernel, lax.axis_size('space'),...  83.3 us

profile of v5, /device:TPU:1, one launch (start us, length us, event | category | flops | bytes accessed | tf_op | source)
XLA Modules:
  0.0 84.7 jit_solution(10300933822292423830)
XLA Ops:
  0.0 0.0 copy-start
  0.0 0.7 copy-done
  0.7 83.3 %gradient.1 = f32[16,32,128]{2,1,0:T(8,128)S(1)} custom-call(bf16[1,4,2,2,3,16,128,128]{7,6,5,4,3,2,1,0:T(8,128)(2,1)} %modes.1, f32[1,4]{1,0:T(1,128)S(1)} %copy-done), custom_call_target="tpu_custom_call" | custom-call | tf_op jit(solution)/shard_map/gradient/pallas_call | solution.py:496
  84.0 0.7 copy.4
Async XLA Ops:
  0.0 0.7 copy-start

commit v6 on v5

--- a/solution.py
+++ b/solution.py
@@ -12,7 +12,7 @@
 PASSES = 3
 MARGIN = 4
 LATE_CHUNKS = 2
-HELD_BACK = 10
+BULK = (6, 3)
 MESH = pl.DeviceIdType.MESH
 
 
@@ -141,8 +141,8 @@
         ]
 
     def bulk(group):
-        split = planes - HELD_BACK
-        first, count = ((0, split), (split, HELD_BACK))[group]
+        first = sum(BULK[:group])
+        count = (*BULK, planes - sum(BULK))[group]
         return send(
             smooth_sum.at[pl.ds(first, count)],
             from_chip.at[pl.ds(first, count)],
@@ -157,7 +157,7 @@
             chip_sum.at[1 - chip, inner + side],
             late_chip.at[side],
             chip_sem,
-            (2 + side,),
+            (3 + side,),
             other_chip,
             me,
         )
@@ -215,15 +215,18 @@
 
     pl.semaphore_wait(barrier, jnp.where(has_far, 2, 1) + core + chip)
 
+    def start_far(c):
+        @pl.when(has_far)
+        def _():
+            halo(c, far).start()
+
     def start_halos(first, last):
         @pl.loop(first, last)
         def _(c):
-            @pl.when(has_far)
-            def _():
-                halo(c, far).start()
-
+            start_far(c + 1)
             halo(c, near).start()
 
+    start_far(0)
     start_halos(0, chunks - LATE_CHUNKS)
 
     def answer(sem, freq_to):
@@ -372,7 +375,8 @@
         early_to_side(1 - near, half).wait_recv()
     smooth_early(1 - chip, pass_on)
     bulk(0).start()
-    start_halos(chunks - LATE_CHUNKS, chunks)
+    start_halos(chunks - LATE_CHUNKS, chunks - 1)
+    halo(chunks - 1, near).start()
     bulk(1).start()
     smooth_early(chip, keep)
 
@@ -384,7 +388,9 @@
 
     @pl.loop(0, 2 * chunks)
     def _(i):
-        c, side = i // 2, lax.rem(i + far, 2)
+        turn = (i == 0) | ((lax.rem(i, 2) == 1) & (i < 2 * chunks - 1))
+        c = (i + 1) // 2 - jnp.where(turn, 0, 1)
+        side = jnp.where(turn, far, near)
         m, part = c // 2, lax.rem(c, 2)
 
         @pl.when((side == near) | has_far)
@@ -394,25 +400,29 @@
         weight = gains[0, m] * (0.25 * factor)
         acc[inner + side] += weight * term(m, part, planes - (planes - 1) * side)
 
-        @pl.when(i == 2 * chunks - 2)
+        @pl.when(i == 2 * chunks - 3)
         def _():
             shift_rows(far_place)
             for copy in late_core(1):
                 copy.start()
 
+        @pl.when(i == 2 * chunks - 2)
+        def _():
+            for copy in late_core(1):
+                copy.wait_recv()
+            add_cores(far_place)
+
+            @pl.when(has_far)
+            def _():
+                for same in (1, 0):
+                    late_to_side(far, same).start()
+
+            late_to_chip(far).start()
+            bulk(2).start()
+
     shift_rows(near_place)
     for copy in late_core(2):
         copy.start()
-    for copy in late_core(1):
-        copy.wait_recv()
-    add_cores(far_place)
-
-    @pl.when(has_far)
-    def _():
-        for same in (1, 0):
-            late_to_side(far, same).start()
-
-    late_to_chip(far).start()
     for copy in late_core(2):
         copy.wait_recv()
     add_cores(near_place)
@@ -420,8 +430,8 @@
     for same in (1, 0):
         late_to_side(near, same).start()
 
-    bulk(0).wait_recv()
-    bulk(1).wait_recv()
+    for group in range(3):
+        bulk(group).wait_recv()
 
     @pl.loop(0, planes)
     def _(p):
@@ -476,8 +486,7 @@
         *early,
         *late_core(1),
         *late_core(2),
-        bulk(0),
-        bulk(1),
+        *(bulk(group) for group in range(3)),
         late_to_chip(far),
         late_to_chip(near),
         *to_side(near),
@@ -523,7 +532,7 @@
             pltpu.SemaphoreType.DMA((mode_count,)),
             pltpu.SemaphoreType.DMA((2, 2, 2 * mode_count)),
             pltpu.SemaphoreType.DMA((2, 3, 2)),
-            pltpu.SemaphoreType.DMA((2, 4)),
+            pltpu.SemaphoreType.DMA((2, 5)),
             pltpu.SemaphoreType.DMA((2, 2, 4)),
             pltpu.SemaphoreType.REGULAR,
             pltpu.SemaphoreType.REGULAR,

time: 85.8 us -> 85.3 us (level)
  no operation moved by 1% of the time
where the time goes in v6:
time: 85.3 us; the launch traced here: 83.8 us
  Pallas kernels  82.5 us (97%)
  local copies, waits for them, and re-layouts  1.36 us (2%)
    pallas_call x1, Pallas kernels, local(): pl.pallas_call(functools.partial(gradient_kernel, lax.axis_size('space'),...  82.5 us

profile of v6, /device:TPU:1, one launch (start us, length us, event | category | flops | bytes accessed | tf_op | source)
XLA Modules:
  0.0 83.8 jit_solution(3716338847357782753)
XLA Ops:
  0.0 0.0 copy-start
  0.0 0.7 copy-done
  0.7 82.5 %gradient.1 = f32[16,32,128]{2,1,0:T(8,128)S(1)} custom-call(bf16[1,4,2,2,3,16,128,128]{7,6,5,4,3,2,1,0:T(8,128)(2,1)} %modes.1, f32[1,4]{1,0:T(1,128)S(1)} %copy-done), custom_call_target="tpu_custom_call" | custom-call | tf_op jit(solution)/shard_map/gradient/pallas_call | solution.py:505
  83.1 0.7 copy.4
Async XLA Ops:
  0.0 0.7 copy-start

commit v7 on v6

--- a/solution.py
+++ b/solution.py
@@ -12,7 +12,7 @@
 PASSES = 3
 MARGIN = 4
 LATE_CHUNKS = 2
-BULK = (6, 3)
+BULK = (6, 3, 4)
 MESH = pl.DeviceIdType.MESH
 
 
@@ -157,7 +157,7 @@
             chip_sum.at[1 - chip, inner + side],
             late_chip.at[side],
             chip_sem,
-            (3 + side,),
+            (4 + side,),
             other_chip,
             me,
         )
@@ -429,13 +429,16 @@
     late_to_chip(near).start()
     for same in (1, 0):
         late_to_side(near, same).start()
+    bulk(3).start()
+
+    def add_bulk(first, last):
+        @pl.loop(first, last)
+        def _(p):
+            out[p] += from_chip[p]
 
     for group in range(3):
         bulk(group).wait_recv()
-
-    @pl.loop(0, planes)
-    def _(p):
-        out[p] += from_chip[p]
+    add_bulk(0, sum(BULK))
 
     def add_late(p, value):
         out[p] += value
@@ -462,6 +465,8 @@
     for same in (1, 0):
         late_to_side(1 - near, same).wait_recv()
     smooth_late(near)
+    bulk(3).wait_recv()
+    add_bulk(sum(BULK), planes)
 
     @pl.loop(0, chunks)
     def _(c):
@@ -486,7 +491,7 @@
         *early,
         *late_core(1),
         *late_core(2),
-        *(bulk(group) for group in range(3)),
+        *(bulk(group) for group in range(4)),
         late_to_chip(far),
         late_to_chip(near),
         *to_side(near),
@@ -532,7 +537,7 @@
             pltpu.SemaphoreType.DMA((mode_count,)),
             pltpu.SemaphoreType.DMA((2, 2, 2 * mode_count)),
             pltpu.SemaphoreType.DMA((2, 3, 2)),
-            pltpu.SemaphoreType.DMA((2, 5)),
+            pltpu.SemaphoreType.DMA((2, 6)),
             pltpu.SemaphoreType.DMA((2, 2, 4)),
             pltpu.SemaphoreType.REGULAR,
             pltpu.SemaphoreType.REGULAR,

time: 85.3 us -> 85.5 us (level)
    pallas_call x1, Pallas kernels: 82.5 us -> 83.3 us  [local(): pl.pallas_call(functools.partial(gradient_kernel, lax.axis_size('space'),...]
where the time goes in v7:
time: 85.5 us; the launch traced here: 84.7 us
  Pallas kernels  83.3 us (97%)
  local copies, waits for them, and re-layouts  1.36 us (2%)
    pallas_call x1, Pallas kernels, local(): pl.pallas_call(functools.partial(gradient_kernel, lax.axis_size('space'),...  83.3 us

profile of v7, /device:TPU:1, one launch (start us, length us, event | category | flops | bytes accessed | tf_op | source)
XLA Modules:
  0.0 84.7 jit_solution(1742682235018233751)
XLA Ops:
  0.0 0.0 copy-start
  0.0 0.7 copy-done
  0.7 83.3 %gradient.1 = f32[16,32,128]{2,1,0:T(8,128)S(1)} custom-call(bf16[1,4,2,2,3,16,128,128]{7,6,5,4,3,2,1,0:T(8,128)(2,1)} %modes.1, f32[1,4]{1,0:T(1,128)S(1)} %copy-done), custom_call_target="tpu_custom_call" | custom-call | tf_op jit(solution)/shard_map/gradient/pallas_call | solution.py:510
  84.0 0.7 copy.4
Async XLA Ops:
  0.0 0.7 copy-start

commit v8 on v7

--- a/solution.py
+++ b/solution.py
@@ -12,7 +12,7 @@
 PASSES = 3
 MARGIN = 4
 LATE_CHUNKS = 2
-BULK = (6, 3, 4)
+BULK = (5, 3, 4)
 MESH = pl.DeviceIdType.MESH
 
 

time: 85.5 us -> 85.5 us (level)
  no operation moved by 1% of the time
where the time goes in v8:
time: 85.5 us; the launch traced here: 84.7 us
  Pallas kernels  83.3 us (97%)
  local copies, waits for them, and re-layouts  1.36 us (2%)
    pallas_call x1, Pallas kernels, local(): pl.pallas_call(functools.partial(gradient_kernel, lax.axis_size('space'),...  83.3 us

profile of v8, /device:TPU:1, one launch (start us, length us, event | category | flops | bytes accessed | tf_op | source)
XLA Modules:
  0.0 84.7 jit_solution(7563237041431167458)
XLA Ops:
  0.0 0.0 copy-start
  0.0 0.7 copy-done
  0.7 83.3 %gradient.1 = f32[16,32,128]{2,1,0:T(8,128)S(1)} custom-call(bf16[1,4,2,2,3,16,128,128]{7,6,5,4,3,2,1,0:T(8,128)(2,1)} %modes.1, f32[1,4]{1,0:T(1,128)S(1)} %copy-done), custom_call_target="tpu_custom_call" | custom-call | tf_op jit(solution)/shard_map/gradient/pallas_call | solution.py:510
  84.0 0.7 copy.4
Async XLA Ops:
  0.0 0.7 copy-start
